TPU v7x, 32 devices: a whole 2x2x4 slice. The times are simulated.
32 devices in a mesh: chain: 8 (over z, core), bond: 4 (over y, x).
Axes of the slice: x: 2, y: 2, z: 4, core: 2. Of those that a mesh axis runs over, the one named last changes fastest.
Arguments:
- sites: bfloat16 [8, 1024, 2048], P('chain', 'bond'), may hold values from -0.1875 to 0.1875
- start: bfloat16 [8, 1024, 1024], P('chain', 'bond'), may hold values from -0.125 to 0.125
- gates: float32 [8, 16], replicated, may hold values from -3 to 3
- bonds: int32 [9], replicated, may hold values from 512 to 1024, as said below
Outputs:
- new_sites: float32 [8, 1024, 2048], P('chain', 'bond')
Inputs may be any that keep to these rules, and one draw needn't show every extreme that they name: bonds[k] is the bond dimension of the cut just left of site k.
All inputs are finite; a program needn't handle non-finite values.
Results may differ from a plain program's by a relative error of at most 0.03.
Values may be sent and summed in bfloat16 or wider, within the bound.
A program may use at most 128 MiB of HBM per device.

v0:
```python
import jax
import jax.numpy as jnp
from jax import lax
from jax.sharding import PartitionSpec as P

ridge_ratio = 0.05


def partner(value, axis, apart):
    return lax.ppermute(value, axis, [(i, i ^ 1 << apart) for i in range(lax.axis_size(axis))])


def shifted_factor(gram_matrix, keep_cols):
    trace_sum = jnp.sum(jnp.diagonal(gram_matrix))
    kept_count = jnp.sum(keep_cols.astype(jnp.float32))
    added = jnp.where(keep_cols, ridge_ratio * trace_sum / kept_count, 1.0)
    return jnp.linalg.cholesky(gram_matrix + jnp.diag(added))


def right_solve(factor, values):
    return lax.linalg.triangular_solve(
        factor, values, left_side=False, lower=True, transpose_a=True
    )


def column_gram(values):
    return lax.dot_general(
        values,
        values,
        (((0,), (0,)), ((), ())),
        precision=lax.Precision.HIGHEST,
        preferred_element_type=jnp.float32,
    )


def local(sites, start, gates, bonds):
    bond_index = lax.axis_index("bond")
    chain_index = lax.axis_index("chain")
    rank_width = start.shape[2]
    local_rows = sites.shape[1]
    own_site = sites[0]
    own_start = start[0]
    is_left = chain_index % 2 == 0
    left_site = jnp.where(is_left, chain_index, chain_index - 1)
    bond_left = bonds[left_site]
    bond_mid = bonds[left_site + 1]
    bond_right = bonds[left_site + 2]
    columns = jnp.arange(rank_width)
    row_global = bond_index * local_rows + jnp.arange(local_rows)
    mid_keep = columns < bond_mid
    right_keep = columns < bond_right
    whole_site, whole_start = (
        lax.all_gather(own_site, "bond", axis=0, tiled=True),
        lax.all_gather(own_start, "bond", axis=0, tiled=True),
    )
    other_site, other_start = partner((whole_site, whole_start), "chain", 0)
    b_full, start_zero, start_one = lax.cond(
        is_left,
        lambda: (other_site, whole_start, other_start),
        lambda: (whole_site, other_start, whole_start),
    )
    other_rows = lax.dynamic_slice_in_dim(other_site, bond_index * local_rows, local_rows, 0)
    a_rows = jnp.where(is_left, own_site, other_rows)
    left_keep = (row_global < bond_left)[:, None] & jnp.tile(mid_keep, 2)[None, :]
    left_used = jnp.where(left_keep, a_rows, jnp.zeros((), jnp.bfloat16))
    pair_keep = jnp.tile(right_keep, 2)[None, :]
    mix_zero = jnp.where(
        pair_keep,
        jnp.dot(left_used[:, :rank_width], b_full, preferred_element_type=jnp.float32),
        0.0,
    )
    mix_one = jnp.where(
        pair_keep,
        jnp.dot(left_used[:, rank_width:], b_full, preferred_element_type=jnp.float32),
        0.0,
    )
    gate_matrix = gates[left_site].reshape(4, 4)

    def theta_for(out_row):
        gate_rows = lax.dynamic_slice_in_dim(gate_matrix, 2 * out_row, 2, 0)
        pieces = []
        for out_col in range(2):
            coeffs = gate_rows[out_col]
            pieces.append(
                coeffs[0] * mix_zero[:, :rank_width]
                + coeffs[1] * mix_zero[:, rank_width:]
                + coeffs[2] * mix_one[:, :rank_width]
                + coeffs[3] * mix_one[:, rank_width:]
            )
        return jnp.concatenate(pieces, axis=1).astype(jnp.bfloat16)

    theta_rows = theta_for(jnp.where(is_left, 0, 1))
    theta_second = theta_for(1)
    image_full = jnp.dot(
        theta_rows[:, :rank_width], start_zero, preferred_element_type=jnp.float32
    ) + jnp.dot(theta_rows[:, rank_width:], start_one, preferred_element_type=jnp.float32)
    image_rows = jnp.where(mid_keep[None, :], image_full, 0.0).astype(jnp.bfloat16)
    summed = lax.psum_scatter(
        lax.dot_general(
            theta_rows, image_rows, (((0,), (0,)), ((), ())), preferred_element_type=jnp.float32
        ).astype(jnp.bfloat16),
        "bond",
        scatter_dimension=0,
        tiled=True,
    ).astype(jnp.float32)
    partner_sum = partner(summed, "chain", 0)
    projected = summed + partner_sum
    projected_all = lax.all_gather(projected, "bond", axis=0, tiled=True)
    factor = shifted_factor(column_gram(projected_all), mid_keep)
    exact_basis = right_solve(factor, projected_all)
    basis_new = exact_basis.astype(jnp.bfloat16)
    upper_rows = jnp.dot(theta_rows, basis_new, preferred_element_type=jnp.float32)
    second_rows = jnp.dot(theta_second, basis_new, preferred_element_type=jnp.float32)
    joined = jnp.concatenate([upper_rows, second_rows], axis=1)
    sum_squares = lax.psum(jnp.sum(joined * joined), "bond")
    mean_square = (
        sum_squares / (2.0 * bond_left.astype(jnp.float32) * bond_mid.astype(jnp.float32)) + 1e-06
    )
    new_left = joined * lax.rsqrt(mean_square)
    column_block = lax.dynamic_slice_in_dim(exact_basis, bond_index * local_rows, local_rows, 1)
    new_right = jnp.sqrt(2.0 * bond_right.astype(jnp.float32)) * column_block.T
    output_rows = jnp.where(is_left, new_left, new_right)
    return output_rows[None]


def solution(mesh):
    placed = (P("chain", "bond", None), P("chain", "bond", None), P(), P())
    return jax.shard_map(
        local, mesh=mesh, in_specs=placed, out_specs=P("chain", "bond", None), check_vma=False
    )
```

profile of v0, /device:TPU:0, one launch (start us, length us, event | category | flops | bytes accessed | tf_op | source)
XLA Modules:
  0.0 767.0 jit_solution(167367669043857130)
XLA Ops:
  8.1 56.5 %all-gather.8.cloned.1.call-done = bf16[1,1024,2048]{2,1,0:T(8,128)(2,1)} async-done(((bf16[1,256,2048]{2,1,0:T(8,128)(2,1)}), bf16[1,1024,2048]{2,1,0:T(8,128)(2,1)}) %all-gather.8.cloned.1.call-update) | async-done | bytes 4194320 | tf_op jit(solution)/shard_map/all_gather | solution.py:53
  64.5 37.0 %all-gather.10.cloned.1.call-done = bf16[1,1024,1024]{2,1,0:T(8,128)(2,1)} async-done(((bf16[1,256,1024]{2,1,0:T(8,128)(2,1)}), bf16[1,1024,1024]{2,1,0:T(8,128)(2,1)}) %all-gather.10.cloned.1.call-update) | async-done | bytes 2097168 | tf_op jit(solution)/shard_map/all_gather | solution.py:54
  136.9 52.2 %reduce-scatter.2.cloned.1.call-done = bf16[512,1024]{1,0:T(8,128)(2,1)} async-done(((bf16[2048,1024]{1,0:T(8,128)(2,1)}), bf16[512,1024]{1,0:T(8,128)(2,1)}) %reduce-scatter.2.cloned.1.call-update) | async-done | bytes 1048592 | tf_op jit(solution)/shard_map/reduce_scatter | solution.py:98
  209.9 75.5 %all-gather.6.cloned.1.call-done = f32[2048,1024]{1,0:T(8,128)} async-done(((f32[512,1024]{1,0:T(8,128)}), f32[2048,1024]{1,0:T(8,128)}) %all-gather.6.cloned.1.call-update) | async-done | bytes 8388624 | tf_op jit(solution)/shard_map/all_gather | solution.py:108
  285.4 31.6 %fusion.111 = f32[1024,1024]{1,0:T(8,128)} fusion(f32[2048,1024]{1,0:T(8,128)} %all-gather.6.cloned.1.call-done), kind=kOutput, calls=%fused_computation.219 | convolution fusion | flops 25769803776 | bytes 12582912 | tf_op jit(solution)/shard_map/dot_general | solution.py:27
  322.4 17.3 %gather_fusion = f32[1024]{0:T(1024)S(1)} fusion(f32[1024,1024]{1,0:T(8,128)} %fusion.111, s32[1024]{0:T(1024)S(1)} %bitcast.136), kind=kCustom, calls=%fused_computation | custom fusion | bytes 16384 | tf_op jit(solution)/shard_map/jit(diagonal)/cond/branch_0_fun/gather | solution.py:14
  348.8 11.7 %cholesky.222 = f32[128,128]{1,0:T(8,128)S(1)} custom-call(f32[128,128]{1,0:T(8,128)S(1)} %cholesky.577), custom_call_target="Cholesky" | custom-call | tf_op jit(solution)/shard_map/jit(cholesky)/cholesky | solution.py:17
  363.0 9.8 %custom-call.62 = f32[1,128,128]{1,2,0:T(8,128)S(1)} custom-call(f32[1,128,128]{2,1,0:T(8,128)S(1)} %get-tuple-element.93), custom_call_target="InvertDiagBlocksLowerTriangular" | custom-call | tf_op jit(solution)/shard_map/jit(cholesky)/cholesky | solution.py:17
  376.8 11.9 %cholesky.243 = f32[128,128]{1,0:T(8,128)S(1)} custom-call(f32[128,128]{1,0:T(8,128)S(1)} %cholesky.581), custom_call_target="Cholesky" | custom-call | tf_op jit(solution)/shard_map/jit(cholesky)/cholesky | solution.py:17
  389.4 9.8 %custom-call.63 = f32[1,128,128]{1,2,0:T(8,128)S(1)} custom-call(f32[1,128,128]{2,1,0:T(8,128)S(1)} %get-tuple-element.90), custom_call_target="InvertDiagBlocksLowerTriangular" | custom-call | tf_op jit(solution)/shard_map/jit(cholesky)/cholesky | solution.py:17
  402.5 11.7 %cholesky.466 = f32[128,128]{1,0:T(8,128)S(1)} custom-call(f32[128,128]{1,0:T(8,128)S(1)} %cholesky.586), custom_call_target="Cholesky" | custom-call | tf_op jit(solution)/shard_map/jit(cholesky)/cholesky | solution.py:17
  415.6 9.8 %custom-call.64 = f32[1,128,128]{1,2,0:T(8,128)S(1)} custom-call(f32[1,128,128]{2,1,0:T(8,128)S(1)} %get-tuple-element.87), custom_call_target="InvertDiagBlocksLowerTriangular" | custom-call | tf_op jit(solution)/shard_map/jit(cholesky)/cholesky | solution.py:17
  428.9 12.1 %cholesky.485 = f32[128,128]{1,0:T(8,128)S(1)} custom-call(f32[128,128]{1,0:T(8,128)S(1)} %cholesky.591), custom_call_target="Cholesky" | custom-call | tf_op jit(solution)/shard_map/jit(cholesky)/cholesky | solution.py:17
  455.6 11.7 %cholesky.504 = f32[128,128]{1,0:T(8,128)S(1)} custom-call(f32[128,128]{1,0:T(8,128)S(1)} %cholesky.596), custom_call_target="Cholesky" | custom-call | tf_op jit(solution)/shard_map/jit(cholesky)/cholesky | solution.py:17
  468.7 10.0 %custom-call.66 = f32[1,128,128]{1,2,0:T(8,128)S(1)} custom-call(f32[1,128,128]{2,1,0:T(8,128)S(1)} %get-tuple-element.81), custom_call_target="InvertDiagBlocksLowerTriangular" | custom-call | tf_op jit(solution)/shard_map/jit(cholesky)/cholesky | solution.py:17
  482.0 11.7 %cholesky.524 = f32[128,128]{1,0:T(8,128)S(1)} custom-call(f32[128,128]{1,0:T(8,128)S(1)} %cholesky.601), custom_call_target="Cholesky" | custom-call | tf_op jit(solution)/shard_map/jit(cholesky)/cholesky | solution.py:17
  507.8 11.9 %cholesky.544 = f32[128,128]{1,0:T(8,128)S(1)} custom-call(f32[128,128]{1,0:T(8,128)S(1)} %cholesky.606), custom_call_target="Cholesky" | custom-call | tf_op jit(solution)/shard_map/jit(cholesky)/cholesky | solution.py:17
  521.0 9.8 %custom-call.68 = f32[1,128,128]{1,2,0:T(8,128)S(1)} custom-call(f32[1,128,128]{2,1,0:T(8,128)S(1)} %get-tuple-element.75), custom_call_target="InvertDiagBlocksLowerTriangular" | custom-call | tf_op jit(solution)/shard_map/jit(cholesky)/cholesky | solution.py:17
  533.4 11.7 %cholesky.562 = f32[128,128]{1,0:T(8,128)S(1)} custom-call(f32[128,128]{1,0:T(8,128)S(1)} %slice_subtract_fusion.20), custom_call_target="Cholesky" | custom-call | tf_op jit(solution)/shard_map/jit(cholesky)/cholesky | solution.py:17
  556.8 27.8 %while.1 = (s32[]{:T(128)}, f32[1024,1024]{1,0:T(8,128)}, s32[8,2]{0,1:T(2,128)S(1)}, f32[8,128,128]{2,1,0:T(8,128)}, s32[]{:T(128)}) while((s32[]{:T(128)}, f32[1024,1024]{1,0:T(8,128)}, s32[8,2]{0,1:T(2,128)S(1)}, f32[8,128,128]{2,1,0:T(8,128)}, s32[]{:T(128)}) %tuple.86), condition=%wide.while_cond, body=%wide.while_body.sunk | while | flops 2 | bytes 132205 | solution.py:21
  584.6 80.5 %custom-call.69 = f32[8,128,128]{1,2,0:T(8,128)} custom-call(f32[8,128,128]{2,1,0:T(8,128)} %get-tuple-element.30), custom_call_target="InvertDiagBlocksLowerTriangular" | custom-call | tf_op jit(solution)/shard_map/triangular_solve | solution.py:21
  699.8 9.9 %fusion.62 = f32[2048,128]{1,0:T(8,128)S(1)} fusion(f32[2048,640]{0,1:T(8,128)S(1)} %get-tuple-element.55, f32[1024,1024]{1,0:T(8,128)} %get-tuple-element.175), kind=kOutput, calls=%fused_computation.101 | convolution fusion | flops 2013265920 | bytes 6619136 | tf_op jit(solution)/shard_map/triangular_solve | solution.py:21
  711.8 11.8 %fusion.58 = f32[2048,128]{1,0:T(8,128)S(1)} fusion(f32[2048,768]{0,1:T(8,128)S(1)} %get-tuple-element.51, f32[1024,1024]{1,0:T(8,128)} %get-tuple-element.175), kind=kOutput, calls=%fused_computation.96 | convolution fusion | flops 2415919104 | bytes 7733248 | tf_op jit(solution)/shard_map/triangular_solve | solution.py:21
  725.5 13.6 %fusion.52 = f32[2048,128]{1,0:T(8,128)S(1)} fusion(f32[2048,896]{0,1:T(8,128)S(1)} %get-tuple-element.47, f32[1024,1024]{1,0:T(8,128)} %get-tuple-element.175), kind=kOutput, calls=%fused_computation.89 | convolution fusion | flops 2818572288 | bytes 8847360 | tf_op jit(solution)/shard_map/triangular_solve | solution.py:21
  (162 shorter events, 222.3 us)
Async XLA Ops:
  6.5 58.0 %all-gather.8.cloned.1.call-start = ((), (), s32[]{:S(2)}) async-start(), calls=%async_computation.3 | async-start | bytes 5242880 | tf_op jit(solution)/shard_map/all_gather | solution.py:53
  7.3 94.3 %all-gather.10.cloned.1.call-start = ((), (), s32[]{:S(2)}) async-start(), calls=%async_computation.4 | async-start | bytes 2621440 | tf_op jit(solution)/shard_map/all_gather | solution.py:54
  8.0 181.2 %reduce-scatter.2.cloned.1.call-start = ((), (), s32[]{:S(2)}) async-start(), calls=%async_computation.1 | async-start | bytes 5242880 | tf_op jit(solution)/shard_map/reduce_scatter | solution.py:98
  64.5 43.1 %collective-permute-start = (bf16[1024,2048]{1,0:T(8,128)(2,1)}, bf16[1024,2048]{1,0:T(8,128)(2,1)}, u32[]{:S(2)}, u32[]{:S(2)}) collective-permute-start(bf16[1024,2048]{1,0:T(8,128)(2,1)} %bitcast.142), channel_id=1, source_target_pairs={{0,4},{4,0},{8,12},{12,8},{16,20},{20,16},{24,28},{28,24},{1,5},{5... | collective-permute-start | bytes 12582920 | tf_op jit(solution)/shard_map/ppermute | solution.py:10
  101.6 6.0 collective-permute-start.1
  107.6 7.7 %copy-start.7 = (bf16[1,256,2048]{2,1,0:T(8,128)(2,1)S(1)}, bf16[1,256,2048]{2,1,0:T(8,128)(2,1)}, u32[]{:S(2)}) copy-start(bf16[1,256,2048]{2,1,0:T(8,128)(2,1)} %param.6) | copy-start | bytes 3145732
  107.6 1.3 copy-start.4
  109.0 4.9 copy-start.2
  109.0 5.1 copy-start.5
  115.4 6.1 copy-start.11
  117.9 3.6 copy-start.12
  122.8 7.9 %copy-start.6 = (f32[256,2048]{1,0:T(8,128)}, f32[256,2048]{1,0:T(8,128)S(1)}, u32[]{:S(2)}) copy-start(f32[256,2048]{1,0:T(8,128)S(1)} %convolution_select_fusion.1) | copy-start | bytes 6291460
  122.8 6.2 copy-start.3
  136.4 149.0 %all-gather.6.cloned.1.call-start = ((), (), s32[]{:S(2)}) async-start(), calls=%async_computation.2 | async-start | bytes 10485760 | tf_op jit(solution)/shard_map/all_gather | solution.py:108
  190.6 4.2 collective-permute-start.2
  346.8 2.0 copy-start.1
  665.1 12.4 %slice-start = ((s8[8388608]{0:T(1024)(128)(4,1)}), s8[4194304]{0:T(1024)(128)(4,1)S(1)}, s32[]{:S(2)}) async-start(s8[8388608]{0:T(1024)(128)(4,1)} %bitcast.137), calls=%async_computation.5 | async-start | bytes 8388608
  670.4 7.1 slice-start.1
  679.7 9.7 %copy-start.8 = (f32[2048,128]{0,1:T(8,128)}, f32[2048,128]{0,1:T(8,128)S(1)}, u32[]{:S(2)}) copy-start(f32[2048,128]{0,1:T(8,128)S(1)} %get-tuple-element.117) | copy-start | bytes 3145732
  741.1 3.2 copy-start
  741.1 3.2 copy-start.9
  741.1 3.2 copy-start.10
Sparse Core Ops, SparseCore 0:
  9.2 55.2 all-gather.7
  66.3 35.1 all-gather.9
  136.5 52.5 reduce-scatter.1
  197.9 87.4 all-gather.5
where the time goes:
time: 775 us; the launch traced here: 767 us
  other arithmetic  292 us (38%)
  waiting for transfers between devices  227 us (29%)
  matrix products  145 us (19%)
  local copies, waits for them, and re-layouts  69.4 us (9%)
  between operations  22.8 us (3%)
  blocking collectives  9.55 us (1%)
    another operation x30, other arithmetic, shifted_factor(): return jnp.linalg.cholesky(gram_matrix + jnp.diag(added))  172 us
    another operation x3, other arithmetic, right_solve(): lax.linalg.triangular_solve(factor, values, left_side=False, lower=True,...  85.3 us
    another operation x15, matrix products, right_solve(): lax.linalg.triangular_solve(factor, values, left_side=False, lower=True,...  75.8 us
    all_gather x1, waiting for transfers between devices, local(): projected_all = lax.all_gather(projected, 'bond', axis=0, tiled=True)  75.5 us
    all_gather x1, waiting for transfers between devices, local(): lax.all_gather(own_site, 'bond', axis=0, tiled=True)  56.5 us
    reduce_scatter x1, waiting for transfers between devices, local(): lax.psum_scatter(lax.dot_general(theta_rows, image_rows, (((0,), (0,)), (...  52.2 us
    all_gather x1, waiting for transfers between devices, local(): lax.all_gather(own_start, 'bond', axis=0, tiled=True)  37 us
    dot_general x1, matrix products, column_gram(): lax.dot_general(values, values, (((0,), (0,)), ((), ())), precision=lax.P...  31.6 us
  transfers between devices with their start and end apart: 7, of which 5 were waited for; matrix products, arithmetic and copies ran while one was open for 2% of the time, Pallas kernels for 0%

commit v1 on v0

--- a/solution.py
+++ b/solution.py
@@ -1,36 +1,118 @@
 import jax
 import jax.numpy as jnp
 from jax import lax
+from jax.experimental import pallas as pl
+from jax.experimental.pallas import tpu as pltpu
 from jax.sharding import PartitionSpec as P
 
 ridge_ratio = 0.05
+BLOCK = 128
+SUB = 8
 
 
 def partner(value, axis, apart):
     return lax.ppermute(value, axis, [(i, i ^ 1 << apart) for i in range(lax.axis_size(axis))])
 
 
-def shifted_factor(gram_matrix, keep_cols):
-    trace_sum = jnp.sum(jnp.diagonal(gram_matrix))
-    kept_count = jnp.sum(keep_cols.astype(jnp.float32))
-    added = jnp.where(keep_cols, ridge_ratio * trace_sum / kept_count, 1.0)
-    return jnp.linalg.cholesky(gram_matrix + jnp.diag(added))
-
-
-def right_solve(factor, values):
-    return lax.linalg.triangular_solve(
-        factor, values, left_side=False, lower=True, transpose_a=True
-    )
-
-
-def column_gram(values):
-    return lax.dot_general(
-        values,
-        values,
-        (((0,), (0,)), ((), ())),
-        precision=lax.Precision.HIGHEST,
-        preferred_element_type=jnp.float32,
-    )
+def halves(x):
+    high = x.astype(jnp.bfloat16)
+    return high, (x - high.astype(jnp.float32)).astype(jnp.bfloat16)
+
+
+def diagonal_inverse(tile):
+    lane = lax.broadcasted_iota(jnp.int32, (SUB, BLOCK), 1)
+    sub = lax.broadcasted_iota(jnp.int32, (SUB, BLOCK), 0)
+    count = BLOCK // SUB
+    rows = [tile[i * SUB : (i + 1) * SUB, :] for i in range(count)]
+    full = (SUB, BLOCK)
+    for b in range(count):
+        base = b * SUB
+        cols = [jnp.broadcast_to(rows[b][:, base + j : base + j + 1], full) for j in range(SUB)]
+        current = rows[b]
+        scale = jnp.zeros(full, jnp.float32)
+        inverses, uppers, finals = [], {}, []
+        for j in range(SUB):
+            pivot = jnp.broadcast_to(cols[j][j : j + 1, :], full)
+            inv = 1.0 / pivot
+            inverses.append(inv)
+            scale = jnp.where(sub == j, pivot, scale)
+            m = jnp.where(sub > j, cols[j] * inv, 0.0)
+            for k in range(j + 1, SUB):
+                uppers[j, k] = jnp.broadcast_to(cols[k][j : j + 1, :], full)
+                cols[k] = cols[k] - m * uppers[j, k]
+            row = jnp.broadcast_to(current[j : j + 1, :], full)
+            row = jnp.where(lane == base + j, 1.0, row)
+            finals.append(jnp.where((lane > base + j) & (lane < base + SUB), 0.0, row))
+            current = jnp.where((lane == base + j) & (sub >= j), jnp.where(sub == j, 1.0, 0.0), current) - m * row
+        inside = (lane >= base) & (lane < base + SUB)
+        for i in range(b + 1, count):
+            held = [jnp.broadcast_to(rows[i][:, base + j : base + j + 1], full) for j in range(SUB)]
+            fresh = jnp.where(inside, 0.0, rows[i])
+            for j in range(SUB):
+                c = held[j] * inverses[j]
+                for k in range(j + 1, SUB):
+                    held[k] = held[k] - c * uppers[j, k]
+                fresh = fresh - c * finals[j]
+            rows[i] = fresh
+        rows[b] = jnp.where(lane <= base + sub, current * lax.rsqrt(scale), 0.0)
+    return jnp.concatenate(rows, axis=0)
+
+
+def factor_kernel(gram_ref, out_ref, right_ref):
+    size = gram_ref.shape[0]
+    count = size // BLOCK
+
+    def copy(i, carry):
+        here = pl.ds(pl.multiple_of(i * BLOCK, BLOCK), BLOCK)
+        out_ref[here, :] = gram_ref[here, :]
+        return carry
+
+    lax.fori_loop(0, count, copy, 0)
+
+    def panel(k, carry):
+        here = pl.ds(pl.multiple_of(k * BLOCK, BLOCK), BLOCK)
+        inverse = diagonal_inverse(out_ref[here, here])
+        inv_high, inv_low = halves(inverse)
+        row_high, row_low = halves(out_ref[here, :])
+        out_ref[here, :] = jnp.dot(
+            jnp.concatenate([inv_high, inv_high, inv_low], axis=1),
+            jnp.concatenate([row_high, row_low, row_high], axis=0),
+            preferred_element_type=jnp.float32,
+        )
+        out_ref[here, here] = inverse
+        high, low = halves(out_ref[here, :])
+        right_ref[0:BLOCK, :] = high
+        right_ref[BLOCK : 2 * BLOCK, :] = low
+        right_ref[2 * BLOCK : 3 * BLOCK, :] = high
+
+        def trailing(i, inner):
+            there = pl.ds(pl.multiple_of(i * BLOCK, BLOCK), BLOCK)
+            left_high, left_low = halves(out_ref[here, there].T)
+            out_ref[there, here] = jnp.zeros((BLOCK, BLOCK), jnp.float32)
+            out_ref[there, :] = out_ref[there, :] - jnp.dot(
+                jnp.concatenate([left_high, left_high, left_low], axis=1),
+                right_ref[...],
+                preferred_element_type=jnp.float32,
+            )
+            return inner
+
+        lax.fori_loop(k + 1, count, trailing, 0)
+        column = lax.broadcasted_iota(jnp.int32, (BLOCK, size), 1)
+        out_ref[here, :] = jnp.where(column < (k + 1) * BLOCK, out_ref[here, :], 0.0)
+        return carry
+
+    lax.fori_loop(0, count, panel, 0)
+
+
+def factor_inverse(shifted):
+    size = shifted.shape[0]
+    return pl.pallas_call(
+        factor_kernel,
+        out_shape=jax.ShapeDtypeStruct((size, size), jnp.float32),
+        in_specs=[pl.BlockSpec(memory_space=pltpu.VMEM)],
+        out_specs=pl.BlockSpec(memory_space=pltpu.VMEM),
+        scratch_shapes=[pltpu.VMEM((3 * BLOCK, size), jnp.bfloat16)],
+    )(shifted)
 
 
 def local(sites, start, gates, bonds):
@@ -95,32 +177,64 @@
         theta_rows[:, :rank_width], start_zero, preferred_element_type=jnp.float32
     ) + jnp.dot(theta_rows[:, rank_width:], start_one, preferred_element_type=jnp.float32)
     image_rows = jnp.where(mid_keep[None, :], image_full, 0.0).astype(jnp.bfloat16)
-    summed = lax.psum_scatter(
-        lax.dot_general(
-            theta_rows, image_rows, (((0,), (0,)), ((), ())), preferred_element_type=jnp.float32
-        ).astype(jnp.bfloat16),
-        "bond",
-        scatter_dimension=0,
-        tiled=True,
-    ).astype(jnp.float32)
-    partner_sum = partner(summed, "chain", 0)
-    projected = summed + partner_sum
-    projected_all = lax.all_gather(projected, "bond", axis=0, tiled=True)
-    factor = shifted_factor(column_gram(projected_all), mid_keep)
-    exact_basis = right_solve(factor, projected_all)
-    basis_new = exact_basis.astype(jnp.bfloat16)
-    upper_rows = jnp.dot(theta_rows, basis_new, preferred_element_type=jnp.float32)
-    second_rows = jnp.dot(theta_second, basis_new, preferred_element_type=jnp.float32)
-    joined = jnp.concatenate([upper_rows, second_rows], axis=1)
-    sum_squares = lax.psum(jnp.sum(joined * joined), "bond")
+    own = lax.dot_general(
+        theta_rows, image_rows, (((0,), (0,)), ((), ())), preferred_element_type=jnp.float32
+    ).astype(jnp.bfloat16)
+    kept_half = jnp.where(is_left, 0, 1)
+    half_rows = own.shape[0] // 2
+    kept = lax.dynamic_slice_in_dim(own, kept_half * half_rows, half_rows, 0)
+    given = lax.dynamic_slice_in_dim(own, (1 - kept_half) * half_rows, half_rows, 0)
+    both = (kept.astype(jnp.float32) + partner(given, "chain", 0).astype(jnp.float32)).astype(jnp.bfloat16)
+    summed = lax.psum_scatter(both, "bond", scatter_dimension=0, tiled=True)
+    own_half = lax.all_gather(summed, "bond", axis=0, tiled=True)
+    other_half = partner(own_half, "chain", 0)
+    projected_all = jnp.concatenate(
+        [jnp.where(is_left, own_half, other_half), jnp.where(is_left, other_half, own_half)], axis=0
+    )
+    gram = lax.dot_general(
+        projected_all, projected_all, (((0,), (0,)), ((), ())), preferred_element_type=jnp.float32
+    )
+    eye = jnp.arange(rank_width)[:, None] == jnp.arange(rank_width)[None, :]
+    trace_sum = jnp.sum(jnp.where(eye, gram, 0.0))
+    added = jnp.where(mid_keep, ridge_ratio * trace_sum / bond_mid.astype(jnp.float32), 1.0)
+    inverse = factor_inverse(gram + jnp.where(eye, added[None, :], 0.0))
+
+    def left_rows():
+        pieces = []
+        for theta in (theta_rows, theta_second):
+            reduced = jnp.dot(theta, projected_all, preferred_element_type=jnp.float32)
+            pieces.append(
+                lax.dot_general(
+                    reduced,
+                    inverse,
+                    (((1,), (1,)), ((), ())),
+                    precision=lax.Precision.HIGH,
+                    preferred_element_type=jnp.float32,
+                )
+            )
+        joined = jnp.concatenate(pieces, axis=1)
+        return joined, jnp.sum(joined * joined)
+
+    def right_rows():
+        block = lax.dynamic_slice_in_dim(inverse, bond_index * local_rows, local_rows, 0)
+        basis_rows = lax.dot_general(
+            block,
+            projected_all.astype(jnp.float32),
+            (((1,), (1,)), ((), ())),
+            precision=lax.Precision.HIGH,
+            preferred_element_type=jnp.float32,
+        )
+        return basis_rows, jnp.float32(0.0)
+
+    rows, squares = lax.cond(is_left, left_rows, right_rows)
+    sum_squares = lax.psum(squares, "bond")
     mean_square = (
         sum_squares / (2.0 * bond_left.astype(jnp.float32) * bond_mid.astype(jnp.float32)) + 1e-06
     )
-    new_left = joined * lax.rsqrt(mean_square)
-    column_block = lax.dynamic_slice_in_dim(exact_basis, bond_index * local_rows, local_rows, 1)
-    new_right = jnp.sqrt(2.0 * bond_right.astype(jnp.float32)) * column_block.T
-    output_rows = jnp.where(is_left, new_left, new_right)
-    return output_rows[None]
+    factor = jnp.where(
+        is_left, lax.rsqrt(mean_square), jnp.sqrt(2.0 * bond_right.astype(jnp.float32))
+    )
+    return (rows * factor)[None]
 
 
 def solution(mesh):

time: 775 us -> 332 us (0.43)
  other arithmetic: 292 us -> 35.2 us
  matrix products: 145 us -> 28.9 us
  waiting for transfers between devices: 227 us -> 171 us
  local copies, waits for them, and re-layouts: 69.4 us -> 17.9 us
  Pallas kernels: 0 us -> 50 us
    another operation x34 -> x1, other arithmetic: 266 us -> 5.35 us  [the longest x30 172 us: shifted_factor(): return jnp.linalg.cholesky(gram_matrix + jnp.diag(added))]
    another operation x29 -> x0, matrix products: 98.9 us -> none  [the longest x15 75.8 us: right_solve(): lax.linalg.triangular_solve(factor, values, left_side=False, lower=True,...]
    pallas_call x0 -> x1, Pallas kernels: none -> 50 us  [factor_inverse(): pl.pallas_call(factor_kernel, out_shape=jax.ShapeDtypeStruct((size, size)...]
    all_gather x1, waiting for transfers between devices: 75.5 us -> 36.9 us  [local(): own_half = lax.all_gather(summed, 'bond', axis=0, tiled=True)]
    another operation x33 -> x0, local copies, waits for them, and re-layouts: 30.4 us -> none
    dot_general x3 -> x5, matrix products: 34.2 us -> 16.7 us  [the longest x1 7.18 us: local(): lax.dot_general(projected_all, projected_all, (((0,), (0,)), ((), ())), p...]
    gather x1 -> x0, local copies, waits for them, and re-layouts: 17.3 us -> none  [shifted_factor(): trace_sum = jnp.sum(jnp.diagonal(gram_matrix))]
    reduce_scatter x1, waiting for transfers between devices: 52.2 us -> 35.1 us  [local(): summed = lax.psum_scatter(both, 'bond', scatter_dimension=0, tiled=True)]
  transfers between devices with their start and end apart: 7 -> 8, of which waited for: 5 -> 5; matrix products, arithmetic and copies ran while one was open for 2% -> 4% of each run, Pallas kernels for 0% -> 0%
where the time goes in v1:
time: 332 us; the launch traced here: 331 us
  waiting for transfers between devices  171 us (52%)
  Pallas kernels  50 us (15%)
  other arithmetic  35.2 us (11%)
  matrix products  28.9 us (9%)
  local copies, waits for them, and re-layouts  17.9 us (5%)
  between operations  16.4 us (5%)
  blocking collectives  10.1 us (3%)
    all_gather x1, waiting for transfers between devices, local(): lax.all_gather(own_site, 'bond', axis=0, tiled=True)  56.5 us
    pallas_call x1, Pallas kernels, factor_inverse(): pl.pallas_call(factor_kernel, out_shape=jax.ShapeDtypeStruct((size, size)...  50 us
    all_gather x1, waiting for transfers between devices, local(): lax.all_gather(own_start, 'bond', axis=0, tiled=True)  37 us
    all_gather x1, waiting for transfers between devices, local(): own_half = lax.all_gather(summed, 'bond', axis=0, tiled=True)  36.9 us
    reduce_scatter x1, waiting for transfers between devices, local(): summed = lax.psum_scatter(both, 'bond', scatter_dimension=0, tiled=True)  35.1 us
    psum x1, blocking collectives, local(): sum_squares = lax.psum(squares, 'bond')  10.1 us
    cond x13, local copies, waits for them, and re-layouts  9.23 us
    dot_general x1, matrix products, local(): lax.dot_general(projected_all, projected_all, (((0,), (0,)), ((), ())), p...  7.18 us
  transfers between devices with their start and end apart: 8, of which 5 were waited for; matrix products, arithmetic and copies ran while one was open for 4% of the time, Pallas kernels for 0%

profile of v1, /device:TPU:0, one launch (start us, length us, event | category | flops | bytes accessed | tf_op | source)
XLA Modules:
  0.0 331.1 jit_solution(82516371598613282)
XLA Ops:
  8.1 56.5 %all-gather.8.cloned.1.call-done = bf16[1,1024,2048]{2,1,0:T(8,128)(2,1)} async-done(((bf16[1,256,2048]{2,1,0:T(8,128)(2,1)}), bf16[1,1024,2048]{2,1,0:T(8,128)(2,1)}) %all-gather.8.cloned.1.call-update) | async-done | bytes 4194320 | tf_op jit(solution)/shard_map/all_gather | solution.py:135
  64.5 37.0 %all-gather.10.cloned.1.call-done = bf16[1,1024,1024]{2,1,0:T(8,128)(2,1)} async-done(((bf16[1,256,1024]{2,1,0:T(8,128)(2,1)}), bf16[1,1024,1024]{2,1,0:T(8,128)(2,1)}) %all-gather.10.cloned.1.call-update) | async-done | bytes 2097168 | tf_op jit(solution)/shard_map/all_gather | solution.py:136
  107.4 9.3 %conditional.2 = (bf16[1024,2048]{1,0:T(8,128)(2,1)}, bf16[1024,1024]{1,0:T(8,128)(2,1)S(1)}, bf16[1024,1024]{1,0:T(8,128)(2,1)}) conditional(s32[]{:T(128)} %convert_element_type.32, (bf16[1024,2048]{1,0:T(8,128)(2,1)}, bf16[1024,1024]{1,0:T(8,128)(2,1)S(1)}, bf16[1024,1024]{1,0:T(8,128)(2,1)}) %tuple.60, (bf16[1024,2048]{1,0:T(8,128)(2,1)}, ...), branch_computations={%region_0.1_spmd, %region_1.2_spmd} | conditional | bytes 41943148 | solution.py:139
  108.8 5.0 %copy.8 = bf16[1024,2048]{1,0:T(8,128)(2,1)} copy(bf16[1024,2048]{1,0:T(8,128)(2,1)} %get-tuple-element.82) | data formatting | bytes 8388608 | tf_op jit(solution)/shard_map/cond
  116.7 2.5 and_select_fusion
  119.2 3.6 %convolution_select_fusion = f32[256,2048]{1,0:T(8,128)S(1)} fusion(bf16[1024,2048]{1,0:T(8,128)(2,1)} %get-tuple-element.43, pred[2048]{0:T(1024)(128)(4,1)S(1)} %broadcast_in_dim.64, bf16[256,2048]{1,0:T(8,128)(2,1)S(1)} %and_select_fusion), kind=kOutput, calls=%fused_computation.11 | convolution fusion | flops 1074266112 | bytes 6817792 | tf_op jit(solution)/shard_map/dot_general | solution.py:156
  124.2 6.3 %add_convert_fusion.4 = (bf16[256,1024]{1,0:T(8,128)(2,1)S(1)}, bf16[256,1024]{1,0:T(8,128)(2,1)S(1)}) fusion(f32[256,2048]{1,0:T(8,128)S(1)} %convolution_select_fusion, f32[256,2048]{1,0:T(8,128)S(1)} %convolution_select_fusion.1, f32[]{:T(128)} %bitcast.9, f32[]{:T(128)} %bitcast.8, f32[]{:T(128)} %bitcast.7, f32[]{:T(128)} %bitcast, f32[]{:T(128)} %bitcast.13, ...), kind=kLoop, calls=%fused_computation.26 | loop fusion | flops 4194304 | bytes 5242912 | tf_op jit(solution)/shard_map/slice | solution.py:177
  132.2 5.6 %convolution_convert_fusion = bf16[2048,1024]{1,0:T(8,128)(2,1)} fusion(f32[256,1024]{1,0:T(8,128)} %fusion.19, bf16[256,1024]{1,0:T(8,128)(2,1)S(1)} %get-tuple-element.56, bf16[1024,1024]{1,0:T(8,128)(2,1)} %copy-done.9, pred[1024]{0:T(1024)(128)(4,1)S(1)} %iota_compare_fusion.1, bf16[256,1024]{1,0:T(8,128)(2,1)S(1)} %get-tuple-element.57), kind=kOutput, calls=%fused_computation.10 | convolution fusion | flops 1615593472 | bytes 8389632 | tf_op jit(solution)/shard_map/dot_general | solution.py:180
  137.8 3.1 constant_dynamic-slice_fusion
  140.9 4.5 %collective-permute-done.2 = bf16[1024,1024]{1,0:T(8,128)(2,1)} collective-permute-done((bf16[1024,1024]{1,0:T(8,128)(2,1)}, bf16[1024,1024]{1,0:T(8,128)(2,1)}, u32[]{:S(2)}, u32[]{:S(2)}) %collective-permute-start.2) | collective-permute-done | bytes 2097184 | tf_op jit(solution)/shard_map/ppermute | solution.py:14
  145.4 4.5 %add_convert_fusion = bf16[1024,1024]{1,0:T(8,128)(2,1)} fusion(bf16[1024,1024]{1,0:T(8,128)(2,1)} %collective-permute-done.2, bf16[2048,1024]{1,0:T(8,128)(2,1)} %convolution_convert_fusion, s32[]{:T(128)S(6)} %select_n.113), kind=kLoop, calls=%fused_computation.9 | loop fusion | flops 4194304 | bytes 6291460 | tf_op jit(solution)/shard_map/convert_element_type | solution.py:187
  150.2 35.1 %reduce-scatter.2.cloned.1.call-done = bf16[256,1024]{1,0:T(8,128)(2,1)} async-done(((bf16[1024,1024]{1,0:T(8,128)(2,1)}), bf16[256,1024]{1,0:T(8,128)(2,1)}) %reduce-scatter.2.cloned.1.call-update) | async-done | bytes 524304 | tf_op jit(solution)/shard_map/reduce_scatter | solution.py:188
  185.3 36.9 %all-gather.6.cloned.1.call-done = bf16[1024,1024]{1,0:T(8,128)(2,1)} async-done(((bf16[256,1024]{1,0:T(8,128)(2,1)}), bf16[1024,1024]{1,0:T(8,128)(2,1)}) %all-gather.6.cloned.1.call-update) | async-done | bytes 2097168 | tf_op jit(solution)/shard_map/all_gather | solution.py:189
  225.7 5.4 %add_convert_fusion.2 = (bf16[256,1024]{1,0:T(8,128)(2,1)S(1)}, bf16[256,1024]{1,0:T(8,128)(2,1)S(1)}) fusion(f32[256,2048]{1,0:T(8,128)S(1)} %convolution_select_fusion, f32[256,2048]{1,0:T(8,128)S(1)} %copy-done.7, f32[]{:T(128)} %bitcast.17, f32[]{:T(128)} %bitcast.16, f32[]{:T(128)} %bitcast.15, f32[]{:T(128)} %bitcast.14, f32[]{:T(128)} %bitcast.21, ...), kind=kLoop, calls=%fused_computation.24 | loop fusion | flops 4194304 | bytes 5242912 | tf_op jit(solution)/shard_map/convert
  233.0 2.1 broadcast_select_fusion.1
  235.2 7.2 %select_reduce_fusion = (f32[]{:T(128)}, f32[1024,1024]{1,0:T(8,128)}) fusion(bf16[1024,1024]{1,0:T(8,128)(2,1)S(1)} %get-tuple-element.55, bf16[1024,1024]{1,0:T(8,128)(2,1)S(1)} %get-tuple-element.54), kind=kOutput, calls=%fused_computation.7 | convolution fusion | flops 4306501632 | bytes 8388612 | tf_op jit(solution)/shard_map/dot_general | solution.py:194
  242.4 2.4 pad_maximum_fusion.1
  246.0 4.9 %select_add_fusion.gram_ref = f32[1024,1024]{1,0:T(8,128)} fusion(f32[1024,1024]{1,0:T(8,128)} %get-tuple-element.78, f32[1024]{0:T(1024)S(1)} %broadcast_select_fusion.2), kind=kLoop, calls=%fused_computation.6 | loop fusion | flops 3145728 | bytes 8392704 | tf_op jit(solution)/shard_map/add | solution.py:200
  250.9 50.0 %shard_map.46 = f32[1024,1024]{1,0:T(8,128)} custom-call(f32[1024,1024]{1,0:T(8,128)} %select_add_fusion.gram_ref), custom_call_target="tpu_custom_call" | custom-call | tf_op jit(solution)/shard_map/pallas_call | solution.py:109
  300.9 11.4 %conditional.3 = (f32[256,2048]{1,0:T(8,128)S(1)}, f32[]{:T(128)}) conditional(s32[]{:T(128)} %convert_element_type.32, (s32[]{:T(128)}, f32[1024,1024]{1,0:T(8,128)}, bf16[2048,1024]{1,0:T(8,128)(2,1)}) %tuple.21, (bf16[256,2048]{1,0:T(8,128)(2,1)S(1)}, bf16[2048,1024]{1,0:T(8,128)(2,1)}, f32[1024,1024]{1,0:T(8,128)}, ...), branch_computations={%region_4.5_spmd, %region_5.7_spmd} | conditional | flops 5370281984 | bytes 62914636 | solution.py:229
  300.9 3.9 %fusion.17 = f32[256,1024]{1,0:T(8,128)S(1)} fusion(bf16[256,2048]{1,0:T(8,128)(2,1)} %get-tuple-element.37, bf16[2048,1024]{1,0:T(8,128)(2,1)} %get-tuple-element.35), kind=kOutput, calls=%fused_computation.46 | convolution fusion | flops 1073741824 | bytes 6291456 | tf_op jit(solution)/shard_map/cond/branch_1_fun/dot_general | solution.py:205
  304.8 2.2 fusion.18
  308.3 2.2 fusion.16
  312.3 10.1 %psum.7 = f32[]{:T(128)} all-reduce(f32[]{:T(128)} %get-tuple-element.47), channel_id=1, replica_groups=mesh['chain'=8,'bond'=4] {'bond'}, use_global_device_ids=true, to_apply=%region_7.8 | all-reduce | flops 1 | bytes 8 | tf_op jit(solution)/shard_map/psum | solution.py:230
  (65 shorter events, 23.0 us)
Async XLA Ops:
  6.5 58.0 %all-gather.8.cloned.1.call-start = ((), (), s32[]{:S(2)}) async-start(), calls=%async_computation.3 | async-start | bytes 5242880 | tf_op jit(solution)/shard_map/all_gather | solution.py:135
  7.3 94.3 %all-gather.10.cloned.1.call-start = ((), (), s32[]{:S(2)}) async-start(), calls=%async_computation.4 | async-start | bytes 2621440 | tf_op jit(solution)/shard_map/all_gather | solution.py:136
  8.0 177.3 %reduce-scatter.2.cloned.1.call-start = ((), (), s32[]{:S(2)}) async-start(), calls=%async_computation.1 | async-start | bytes 2621440 | tf_op jit(solution)/shard_map/reduce_scatter | solution.py:188
  64.5 42.9 %collective-permute-start = (bf16[1024,2048]{1,0:T(8,128)(2,1)}, bf16[1024,2048]{1,0:T(8,128)(2,1)}, u32[]{:S(2)}, u32[]{:S(2)}) collective-permute-start(bf16[1024,2048]{1,0:T(8,128)(2,1)} %bitcast.45), channel_id=1, source_target_pairs={{0,4},{4,0},{8,12},{12,8},{16,20},{20,16},{24,28},{28,24},{1,5},{5... | collective-permute-start | bytes 12582920 | tf_op jit(solution)/shard_map/ppermute | solution.py:14
  101.6 5.9 %collective-permute-start.1 = (bf16[1024,1024]{1,0:T(8,128)(2,1)}, bf16[1024,1024]{1,0:T(8,128)(2,1)S(1)}, u32[]{:S(2)}, u32[]{:S(2)}) collective-permute-start(bf16[1024,1024]{1,0:T(8,128)(2,1)} %bitcast.42), channel_id=1, source_target_pairs={{0,4},{4,0},{8,12},{12,8},{16,20},{20,16},{24,28},{28,24},{1,5},{5... | collective-permute-start | bytes 6291464 | tf_op jit(solution)/shard_map/ppermute | solution.py:14
  107.4 9.3 %copy-start.8 = (bf16[1,256,2048]{2,1,0:T(8,128)(2,1)S(1)}, bf16[1,256,2048]{2,1,0:T(8,128)(2,1)}, u32[]{:S(2)}) copy-start(bf16[1,256,2048]{2,1,0:T(8,128)(2,1)} %param.8) | copy-start | bytes 3145732
  107.5 1.3 copy-start.4
  108.8 5.0 %copy-start.2 = (bf16[1024,1024]{1,0:T(8,128)(2,1)S(1)}, bf16[1024,1024]{1,0:T(8,128)(2,1)}, u32[]{:S(2)}) copy-start(bf16[1024,1024]{1,0:T(8,128)(2,1)} %get-tuple-element.83) | copy-start | bytes 6291460 | tf_op jit(solution)/shard_map/cond
  113.7 1.6 copy-start.5
  116.7 6.2 %copy-start.9 = (bf16[1024,1024]{1,0:T(8,128)(2,1)}, bf16[1024,1024]{1,0:T(8,128)(2,1)S(1)}, u32[]{:S(2)}) copy-start(bf16[1024,1024]{1,0:T(8,128)(2,1)S(1)} %get-tuple-element.44) | copy-start | bytes 6291460
  119.2 3.6 %copy-start.12 = (bf16[1024,2048]{1,0:T(8,128)(2,1)S(1)}, bf16[1024,2048]{1,0:T(8,128)(2,1)}, u32[]{:S(2)}) copy-start(bf16[1024,2048]{1,0:T(8,128)(2,1)} %get-tuple-element.43) | copy-start | bytes 12582916
  124.2 6.3 %copy-start.6 = (f32[256,2048]{1,0:T(8,128)}, f32[256,2048]{1,0:T(8,128)S(1)}, u32[]{:S(2)}) copy-start(f32[256,2048]{1,0:T(8,128)S(1)} %convolution_select_fusion.1) | copy-start | bytes 6291460
  124.2 6.3 %copy-start.3 = (bf16[1024,1024]{1,0:T(8,128)(2,1)S(1)}, bf16[1024,1024]{1,0:T(8,128)(2,1)}, u32[]{:S(2)}) copy-start(bf16[1024,1024]{1,0:T(8,128)(2,1)} %get-tuple-element.45) | copy-start | bytes 6291460
  140.9 4.5 %collective-permute-start.2 = (bf16[1024,1024]{1,0:T(8,128)(2,1)}, bf16[1024,1024]{1,0:T(8,128)(2,1)}, u32[]{:S(2)}, u32[]{:S(2)}) collective-permute-start(bf16[1024,1024]{1,0:T(8,128)(2,1)} %constant_dynamic-slice_fusion), channel_id=1, source_target_pairs={{0,4},{4,0},{8,12},{12,8},{16,20},{20,16},{24,28},{28,24},{1,5},{5... | collective-permute-start | bytes 6291464 | tf_op jit(solution)/shard_map/ppermute | solution.py:14
  149.9 72.2 %all-gather.6.cloned.1.call-start = ((), (), s32[]{:S(2)}) async-start(), calls=%async_computation.2 | async-start | bytes 2621440 | tf_op jit(solution)/shard_map/all_gather | solution.py:189
  222.2 10.0 %collective-permute-start.3 = (bf16[1024,1024]{1,0:T(8,128)(2,1)}, bf16[1024,1024]{1,0:T(8,128)(2,1)}, u32[]{:S(2)}, u32[]{:S(2)}) collective-permute-start(bf16[1024,1024]{1,0:T(8,128)(2,1)} %all-gather.6.cloned.1.call-done), channel_id=1, source_target_pairs={{0,4},{4,0},{8,12},{12,8},{16,20},{20,16},{24,28},{28,24},{1,5},{5... | collective-permute-start | bytes 6291464 | tf_op jit(solution)/shard_map/ppermute | solution.py:14
  224.0 1.7 copy-start.7
  231.1 2.0 copy-start.10
  250.9 50.0 %copy-start.11 = (bf16[256,2048]{1,0:T(8,128)(2,1)S(1)}, bf16[256,2048]{1,0:T(8,128)(2,1)}, u32[]{:S(2)}) copy-start(bf16[256,2048]{1,0:T(8,128)(2,1)} %pad_maximum_fusion.2) | copy-start | bytes 3145732
  300.9 3.9 %copy-start = (f32[1024,1024]{1,0:T(8,128)S(1)}, f32[1024,1024]{1,0:T(8,128)}, u32[]{:S(2)}) copy-start(f32[1024,1024]{1,0:T(8,128)} %get-tuple-element.36) | copy-start | bytes 12582916 | tf_op jit(solution)/shard_map/cond
  304.8 2.2 copy-start.1
Sparse Core Ops, SparseCore 0:
  9.2 55.2 all-gather.7
  66.3 35.1 all-gather.9
  150.1 35.1 reduce-scatter.1
  187.0 35.1 all-gather.5

commit v2 on v1

--- a/solution.py
+++ b/solution.py
@@ -115,6 +115,205 @@
     )(shifted)
 
 
+MESH = pl.DeviceIdType.MESH
+
+
+class Links:
+    def __init__(self, send_sem, recv_sem):
+        self.chain, self.me = lax.axis_index("chain"), lax.axis_index("bond")
+        self.core = self.chain % 2
+        self.near = self.me + 1 - 2 * (self.me % 2)
+        self.far = (self.me + 2) % 4
+        self.across = 3 - self.me
+        self.x, self.y, self.d = (self.chain, self.near), (self.chain, self.far), (self.chain, self.across)
+        self.mate = (self.chain + 1 - 2 * self.core, self.me)
+        self.send_sem, self.recv_sem, self.copies = send_sem, recv_sem, []
+
+    def greet(self, others):
+        barrier = pltpu.get_barrier_semaphore()
+        for other in others:
+            pl.semaphore_signal(barrier, inc=1, device_id=other, device_id_type=MESH)
+        pl.semaphore_wait(barrier, len(others))
+
+    def send(self, source, target, device):
+        slot = len(self.copies)
+        copy = pltpu.make_async_remote_copy(
+            src_ref=source,
+            dst_ref=target,
+            send_sem=self.send_sem.at[slot],
+            recv_sem=self.recv_sem.at[slot],
+            device_id=device,
+            device_id_type=MESH,
+        )
+        copy.start()
+        self.copies.append(copy)
+        return copy
+
+    def spread(self, first_own, second_own, first, second):
+        s0 = self.send(second_own, second(self.me), self.x)
+        f0 = self.send(first_own, first(self.me), self.y)
+        f1 = self.send(first_own, first(self.me), self.x)
+        s1 = self.send(second_own, second(self.me), self.y)
+        f0.wait_recv()
+        f2 = self.send(first(self.far), first(self.far), self.x)
+        late = [self.send(first(self.far), first(self.far), self.mate)]
+        s0.wait_recv()
+        s2 = self.send(second(self.near), second(self.near), self.y)
+        late.append(self.send(second(self.near), second(self.near), self.mate))
+        f1.wait_recv()
+        late.append(self.send(first(self.near), first(self.near), self.mate))
+        s1.wait_recv()
+        late.append(self.send(second(self.far), second(self.far), self.mate))
+        f2.wait_recv()
+        late.append(self.send(first(self.across), first(self.across), self.mate))
+        s2.wait_recv()
+        late.append(self.send(second(self.across), second(self.across), self.mate))
+        for copy in late:
+            copy.wait_recv()
+
+    def drain(self):
+        for copy in self.copies:
+            copy.wait_send()
+
+
+def gather_kernel(b_ref, s_ref, b_out, s_out, send_sem, recv_sem, local_sem):
+    links = Links(send_sem, recv_sem)
+    links.greet((links.x, links.y, links.mate))
+    core, me = links.core, links.me
+    kept_b = pltpu.make_async_copy(b_ref, b_out.at[me], local_sem.at[0])
+    kept_s = pltpu.make_async_copy(s_ref, s_out.at[core, me], local_sem.at[1])
+    own = links.send(s_ref, s_out.at[core, me], links.mate)
+    kept_b.start()
+    kept_s.start()
+    links.spread(
+        b_ref.at[core], s_ref, lambda i: b_out.at[i, core], lambda i: s_out.at[core, i]
+    )
+    own.wait_recv()
+    links.drain()
+    kept_b.wait()
+    kept_s.wait()
+
+
+def gather_pair(b_rows, own_start):
+    rows, wide = b_rows.shape
+    width = own_start.shape[1]
+    n = lax.axis_size("bond")
+    b_full, starts = pl.pallas_call(
+        gather_kernel,
+        out_shape=(
+            jax.ShapeDtypeStruct((n, 2, rows // 2, wide), b_rows.dtype),
+            jax.ShapeDtypeStruct((2, n, rows, width), own_start.dtype),
+        ),
+        in_specs=[pl.BlockSpec(memory_space=pltpu.VMEM)] * 2,
+        out_specs=(pl.BlockSpec(memory_space=pl.ANY),) * 2,
+        scratch_shapes=[
+            pltpu.SemaphoreType.DMA((13,)),
+            pltpu.SemaphoreType.DMA((13,)),
+            pltpu.SemaphoreType.DMA((2,)),
+        ],
+        compiler_params=pltpu.CompilerParams(collective_id=0, has_side_effects=True),
+    )(b_rows.reshape(2, rows // 2, wide), own_start)
+    return b_full.reshape(n * rows, wide), starts.reshape(2, n * rows, width)
+
+
+def reduce_kernel(own_ref, out_ref, inc, acc, one, two, send_sem, recv_sem):
+    links = Links(send_sem, recv_sem)
+    links.greet((links.x, links.y, links.mate))
+    core, me, near, far, across = links.core, links.me, links.near, links.far, links.across
+    half = own_ref.shape[2] // 2
+    low, high = pl.ds(0, half), pl.ds(half, half)
+    order = (across, near, far, me)
+    swaps = [links.send(own_ref.at[1 - core, i], inc.at[i], links.mate) for i in order]
+
+    def merge(position):
+        i = order[position]
+        swaps[position].wait_recv()
+        acc[i] = (own_ref[core, i].astype(jnp.float32) + inc[i].astype(jnp.float32)).astype(jnp.bfloat16)
+
+    merge(0)
+    x1 = links.send(acc.at[across, low], one.at[0, 1], links.x)
+    y1 = links.send(acc.at[across, high], one.at[1, 1], links.y)
+    merge(1)
+    x0 = links.send(acc.at[near, low], one.at[0, 0], links.x)
+    merge(2)
+    y0 = links.send(acc.at[far, high], one.at[1, 0], links.y)
+    merge(3)
+    x1.wait_recv()
+    two[2] = (acc[far, low].astype(jnp.float32) + one[0, 1].astype(jnp.float32)).astype(jnp.bfloat16)
+    y2 = links.send(two.at[2], two.at[0], links.y)
+    y1.wait_recv()
+    two[3] = (acc[near, high].astype(jnp.float32) + one[1, 1].astype(jnp.float32)).astype(jnp.bfloat16)
+    x2 = links.send(two.at[3], two.at[1], links.x)
+    x0.wait_recv()
+    y2.wait_recv()
+    out_ref[core, me, low] = (
+        acc[me, low].astype(jnp.float32) + one[0, 0].astype(jnp.float32) + two[0].astype(jnp.float32)
+    ).astype(jnp.bfloat16)
+    y0.wait_recv()
+    x2.wait_recv()
+    out_ref[core, me, high] = (
+        acc[me, high].astype(jnp.float32) + one[1, 0].astype(jnp.float32) + two[1].astype(jnp.float32)
+    ).astype(jnp.bfloat16)
+    own = links.send(out_ref.at[core, me], out_ref.at[core, me], links.mate)
+    links.spread(
+        out_ref.at[core, me, low],
+        out_ref.at[core, me, high],
+        lambda i: out_ref.at[core, i, low],
+        lambda i: out_ref.at[core, i, high],
+    )
+    own.wait_recv()
+    links.drain()
+
+
+def reduce_pair(own):
+    total, width = own.shape
+    n = lax.axis_size("bond")
+    rows = total // (2 * n)
+    whole = pl.pallas_call(
+        reduce_kernel,
+        out_shape=jax.ShapeDtypeStruct((2, n, rows, width), own.dtype),
+        in_specs=[pl.BlockSpec(memory_space=pltpu.VMEM)],
+        out_specs=pl.BlockSpec(memory_space=pltpu.VMEM),
+        scratch_shapes=[
+            pltpu.VMEM((n, rows, width), own.dtype),
+            pltpu.VMEM((n, rows, width), own.dtype),
+            pltpu.VMEM((2, 2, rows // 2, width), own.dtype),
+            pltpu.VMEM((4, rows // 2, width), own.dtype),
+            pltpu.SemaphoreType.DMA((23,)),
+            pltpu.SemaphoreType.DMA((23,)),
+        ],
+        compiler_params=pltpu.CompilerParams(collective_id=1, has_side_effects=True),
+    )(own.reshape(2, n, rows, width))
+    return whole.reshape(total, width)
+
+
+def total_kernel(value_ref, out_ref, held, send_sem, recv_sem):
+    links = Links(send_sem, recv_sem)
+    others = (links.x, links.y, links.d)
+    links.greet(others)
+    copies = [links.send(value_ref, held.at[i], other) for i, other in enumerate(others)]
+    for copy in copies:
+        copy.wait_recv()
+    out_ref[...] = (value_ref[...] + held[2]) + (held[0] + held[1])
+    links.drain()
+
+
+def total_of(value):
+    shape = (8, 128)
+    return pl.pallas_call(
+        total_kernel,
+        out_shape=jax.ShapeDtypeStruct(shape, jnp.float32),
+        in_specs=[pl.BlockSpec(memory_space=pltpu.VMEM)],
+        out_specs=pl.BlockSpec(memory_space=pltpu.VMEM),
+        scratch_shapes=[
+            pltpu.VMEM((3,) + shape, jnp.float32),
+            pltpu.SemaphoreType.DMA((3,)),
+            pltpu.SemaphoreType.DMA((3,)),
+        ],
+        compiler_params=pltpu.CompilerParams(collective_id=2, has_side_effects=True),
+    )(jnp.full(shape, value, jnp.float32))[0, 0]
+
+
 def local(sites, start, gates, bonds):
     bond_index = lax.axis_index("bond")
     chain_index = lax.axis_index("chain")
@@ -131,18 +330,20 @@
     row_global = bond_index * local_rows + jnp.arange(local_rows)
     mid_keep = columns < bond_mid
     right_keep = columns < bond_right
-    whole_site, whole_start = (
-        lax.all_gather(own_site, "bond", axis=0, tiled=True),
-        lax.all_gather(own_start, "bond", axis=0, tiled=True),
-    )
-    other_site, other_start = partner((whole_site, whole_start), "chain", 0)
-    b_full, start_zero, start_one = lax.cond(
-        is_left,
-        lambda: (other_site, whole_start, other_start),
-        lambda: (whole_site, other_start, whole_start),
-    )
-    other_rows = lax.dynamic_slice_in_dim(other_site, bond_index * local_rows, local_rows, 0)
+    other_rows = partner(own_site, "chain", 0)
     a_rows = jnp.where(is_left, own_site, other_rows)
+    b_rows = jnp.where(is_left, other_rows, own_site)
+    square = lax.axis_size("bond") == 4
+    if square:
+        b_full, starts = gather_pair(b_rows, own_start)
+    else:
+        b_full = lax.all_gather(b_rows, "bond", axis=0, tiled=True)
+        whole_start = lax.all_gather(own_start, "bond", axis=0, tiled=True)
+        other_start = partner(whole_start, "chain", 0)
+        starts = jnp.stack(
+            [jnp.where(is_left, whole_start, other_start), jnp.where(is_left, other_start, whole_start)]
+        )
+    start_zero, start_one = starts[0], starts[1]
     left_keep = (row_global < bond_left)[:, None] & jnp.tile(mid_keep, 2)[None, :]
     left_used = jnp.where(left_keep, a_rows, jnp.zeros((), jnp.bfloat16))
     pair_keep = jnp.tile(right_keep, 2)[None, :]
@@ -180,17 +381,20 @@
     own = lax.dot_general(
         theta_rows, image_rows, (((0,), (0,)), ((), ())), preferred_element_type=jnp.float32
     ).astype(jnp.bfloat16)
-    kept_half = jnp.where(is_left, 0, 1)
-    half_rows = own.shape[0] // 2
-    kept = lax.dynamic_slice_in_dim(own, kept_half * half_rows, half_rows, 0)
-    given = lax.dynamic_slice_in_dim(own, (1 - kept_half) * half_rows, half_rows, 0)
-    both = (kept.astype(jnp.float32) + partner(given, "chain", 0).astype(jnp.float32)).astype(jnp.bfloat16)
-    summed = lax.psum_scatter(both, "bond", scatter_dimension=0, tiled=True)
-    own_half = lax.all_gather(summed, "bond", axis=0, tiled=True)
-    other_half = partner(own_half, "chain", 0)
-    projected_all = jnp.concatenate(
-        [jnp.where(is_left, own_half, other_half), jnp.where(is_left, other_half, own_half)], axis=0
-    )
+    if square:
+        projected_all = reduce_pair(own)
+    else:
+        kept_half = jnp.where(is_left, 0, 1)
+        half_rows = own.shape[0] // 2
+        kept = lax.dynamic_slice_in_dim(own, kept_half * half_rows, half_rows, 0)
+        given = lax.dynamic_slice_in_dim(own, (1 - kept_half) * half_rows, half_rows, 0)
+        both = (kept.astype(jnp.float32) + partner(given, "chain", 0).astype(jnp.float32)).astype(jnp.bfloat16)
+        summed = lax.psum_scatter(both, "bond", scatter_dimension=0, tiled=True)
+        own_half = lax.all_gather(summed, "bond", axis=0, tiled=True)
+        other_half = partner(own_half, "chain", 0)
+        projected_all = jnp.concatenate(
+            [jnp.where(is_left, own_half, other_half), jnp.where(is_left, other_half, own_half)], axis=0
+        )
     gram = lax.dot_general(
         projected_all, projected_all, (((0,), (0,)), ((), ())), preferred_element_type=jnp.float32
     )
@@ -227,7 +431,7 @@
         return basis_rows, jnp.float32(0.0)
 
     rows, squares = lax.cond(is_left, left_rows, right_rows)
-    sum_squares = lax.psum(squares, "bond")
+    sum_squares = total_of(squares) if square else lax.psum(squares, "bond")
     mean_square = (
         sum_squares / (2.0 * bond_left.astype(jnp.float32) * bond_mid.astype(jnp.float32)) + 1e-06
     )

time: 332 us -> 220 us (0.66)
  waiting for transfers between devices: 171 us -> 0.01 us
  Pallas kernels: 50 us -> 145 us
  between operations: 16.4 us -> 3.43 us
  blocking collectives: 10.1 us -> 0 us
  other arithmetic: 35.2 us -> 27.1 us
  local copies, waits for them, and re-layouts: 17.9 us -> 10.3 us
  matrix products: 28.9 us -> 32.3 us
    all_gather x3 -> x0, waiting for transfers between devices: 130 us -> none  [the longest x1 56.5 us: local(): lax.all_gather(own_site, 'bond', axis=0, tiled=True)]
    pallas_call x0 -> x3, Pallas kernels: none -> 95.1 us  [the longest x1 46.1 us: reduce_pair(): pl.pallas_call(reduce_kernel, out_shape=jax.ShapeDtypeStruct((2, n, rows,...]
    reduce_scatter x1 -> x0, waiting for transfers between devices: 35.1 us -> none  [local(): summed = lax.psum_scatter(both, 'bond', scatter_dimension=0, tiled=True)]
    psum x1 -> x0, blocking collectives: 10.1 us -> none  [local(): sum_squares = lax.psum(squares, 'bond')]
    cond x13 -> x6, local copies, waits for them, and re-layouts: 9.23 us -> 1.03 us
    ppermute x4 -> x1, waiting for transfers between devices: 4.51 us -> 0.01 us  [partner(): lax.ppermute(value, axis, [(i, i ^ 1 << apart) for i in range(lax.axis_si...]
    convert_element_type x1 -> x0, other arithmetic: 4.5 us -> none  [local(): (kept.astype(jnp.float32) + partner(given, 'chain', 0).astype(jnp.float32...]
    dot_general x1, matrix products: 7.18 us -> 10.6 us  [local(): lax.dot_general(projected_all, projected_all, (((0,), (0,)), ((), ())), p...]
  transfers between devices with their start and end apart: 8 -> 1, of which waited for: 5 -> 0; matrix products, arithmetic and copies ran while one was open for 4% -> 3% of each run, Pallas kernels for 0% -> 0%
where the time goes in v2:
time: 220 us; the launch traced here: 219 us
  Pallas kernels  145 us (66%)
  matrix products  32.3 us (15%)
  other arithmetic  27.1 us (12%)
  local copies, waits for them, and re-layouts  10.3 us (5%)
  between operations  3.43 us (2%)
    pallas_call x1, Pallas kernels, factor_inverse(): pl.pallas_call(factor_kernel, out_shape=jax.ShapeDtypeStruct((size, size)...  49.9 us
    pallas_call x1, Pallas kernels, reduce_pair(): pl.pallas_call(reduce_kernel, out_shape=jax.ShapeDtypeStruct((2, n, rows,...  46.1 us
    pallas_call x1, Pallas kernels, gather_pair(): pl.pallas_call(gather_kernel, out_shape=(jax.ShapeDtypeStruct((n, 2, rows...  43.1 us
    dot_general x1, matrix products, local(): lax.dot_general(projected_all, projected_all, (((0,), (0,)), ((), ())), p...  10.6 us
    another operation x1, other arithmetic  7.14 us
    pallas_call x1, Pallas kernels, total_of(): pl.pallas_call(total_kernel, out_shape=jax.ShapeDtypeStruct(shape, jnp.fl...  5.92 us
    dot_general x1, matrix products, local(): lax.dot_general(theta_rows, image_rows, (((0,), (0,)), ((), ())), preferr...  5.64 us
    slice x1, other arithmetic, local(): theta_rows[:, rank_width:]  5.38 us
  transfers between devices with their start and end apart: 1, of which 0 were waited for; matrix products, arithmetic and copies ran while one was open for 3% of the time, Pallas kernels for 0%

profile of v2, /device:TPU:0, one launch (start us, length us, event | category | flops | bytes accessed | tf_op | source)
XLA Modules:
  0.0 219.3 jit_solution(12026562871747204925)
XLA Ops:
  0.5 1.4 fusion.15
  4.3 1.3 fusion.11
  9.0 2.9 %and_select_fusion = (bf16[256,2048]{1,0:T(8,128)(2,1)S(1)}, bf16[256,2048]{1,0:T(8,128)(2,1)}) fusion(bf16[256,2048]{1,0:T(8,128)(2,1)S(1)} %collective-permute-done, pred[]{:T(512)S(6)} %eq.24, pred[2048]{0:T(1024)(128)(4,1)S(1)} %and.24, pred[256]{0:T(512)(128)(4,1)S(1)} %add_compare_fusion, bf16[1,256,2048]{2,1,0:T(8,128)(2,1)} %param.6), kind=kLoop, calls=%fused_computation.13 | loop fusion | flops 2097152 | bytes 4196609 | tf_op jit(solution)/shard_map/jit(_where)/select_n | solution.py:348
  11.9 43.1 %shard_map.46 = (bf16[4,2,128,2048]{3,2,1,0:T(8,128)(2,1)}, bf16[2,4,256,1024]{3,2,1,0:T(8,128)(2,1)}) custom-call(bf16[2,128,2048]{2,1,0:T(8,128)(2,1)} %bitcast.60, bf16[256,1024]{1,0:T(8,128)(2,1)} %bitcast.63), custom_call_target="tpu_custom_call" | custom-call | tf_op jit(solution)/shard_map/pallas_call | solution.py:201
  55.1 3.6 %convolution_select_fusion = f32[256,2048]{1,0:T(8,128)S(1)} fusion(bf16[1024,2048]{1,0:T(8,128)(2,1)} %bitcast.64, pred[2048]{0:T(1024)(128)(4,1)S(1)} %broadcast_in_dim.67, bf16[256,2048]{1,0:T(8,128)(2,1)S(1)} %get-tuple-element.44), kind=kOutput, calls=%fused_computation.10 | convolution fusion | flops 1074266112 | bytes 6817792 | tf_op jit(solution)/shard_map/dot_general | solution.py:357
  58.7 1.3 convolution_select_fusion.1
  60.9 1.8 fusion.12
  62.7 5.4 %add_convert_fusion.2 = (bf16[256,1024]{1,0:T(8,128)(2,1)S(1)}, bf16[256,1024]{1,0:T(8,128)(2,1)S(1)}) fusion(f32[256,2048]{1,0:T(8,128)S(1)} %convolution_select_fusion, f32[256,2048]{1,0:T(8,128)S(1)} %convolution_select_fusion.1, f32[]{:T(128)} %bitcast.14, f32[]{:T(128)} %bitcast.13, f32[]{:T(128)} %bitcast.12, f32[]{:T(128)} %bitcast.11, f32[]{:T(128)} %bitcast.10, ...), kind=kLoop, calls=%fused_computation.21 | loop fusion | flops 4194304 | bytes 5242912 | tf_op jit(solution)/shard_map/slice | solution.py:379
  68.1 1.7 fusion.20
  69.8 5.6 %convolution_convert_fusion = bf16[2048,1024]{1,0:T(8,128)(2,1)} fusion(f32[256,1024]{1,0:T(8,128)} %fusion.20, bf16[256,1024]{1,0:T(8,128)(2,1)S(1)} %get-tuple-element.42, bf16[1024,1024]{1,0:T(8,128)(2,1)} %bitcast.61, pred[1024]{0:T(1024)(128)(4,1)S(1)} %iota_compare_fusion.1, bf16[256,1024]{1,0:T(8,128)(2,1)S(1)} %get-tuple-element.43), kind=kOutput, calls=%fused_computation.9 | convolution fusion | flops 1615593472 | bytes 8389632 | tf_op jit(solution)/shard_map/dot_general | solution.py:381
  75.4 46.1 %shard_map.47 = bf16[2,4,256,1024]{3,2,1,0:T(8,128)(2,1)} custom-call(bf16[2,4,256,1024]{3,2,1,0:T(8,128)(2,1)} %bitcast.59), custom_call_target="tpu_custom_call" | custom-call | tf_op jit(solution)/shard_map/pallas_call | solution.py:272
  121.5 10.6 %fusion.3 = (f32[]{:T(128)}, f32[1024,1024,1,1]{1,0,3,2:T(8,128)}) fusion(bf16[2,4,256,1024]{3,2,1,0:T(8,128)(2,1)} %shard_map.47), kind=kOutput, calls=%fused_computation.7 | convolution fusion | flops 4298113024 | bytes 8388612 | tf_op jit(solution)/shard_map/dot_general | solution.py:398
  133.4 5.0 %bitcast_add_fusion.gram_ref = f32[1024,1024]{1,0:T(8,128)} fusion(f32[1024,1024,1,1]{1,0,3,2:T(8,128)} %get-tuple-element.66, f32[1024]{0:T(1024)S(1)} %broadcast_select_fusion.1), kind=kLoop, calls=%fused_computation.5 | loop fusion | flops 3145728 | bytes 8392704 | tf_op jit(solution)/shard_map/add | solution.py:404
  138.5 49.9 %shard_map.48 = f32[1024,1024]{1,0:T(8,128)} custom-call(f32[1024,1024]{1,0:T(8,128)} %bitcast_add_fusion.gram_ref), custom_call_target="tpu_custom_call" | custom-call | tf_op jit(solution)/shard_map/pallas_call | solution.py:109
  188.3 7.1 %add_convert_fusion.1 = (bf16[256,1024]{1,0:T(8,128)(2,1)S(1)}, bf16[256,1024]{1,0:T(8,128)(2,1)S(1)}) fusion(f32[256,2048]{1,0:T(8,128)S(1)} %convolution_select_fusion, f32[256,2048]{1,0:T(8,128)} %copy-done.2, f32[]{:T(128)} %bitcast.25, f32[]{:T(128)} %bitcast.24, f32[]{:T(128)} %bitcast.23, f32[]{:T(128)} %bitcast.22, f32[]{:T(128)} %bitcast.29, ...), kind=kLoop, calls=%fused_computation.20 | loop fusion | flops 4194304 | bytes 5242912 | tf_op jit(solution)/shard_map/convert
  195.5 1.6 pad_maximum_fusion.1
  197.1 12.4 %conditional.1 = (f32[256,2048]{1,0:T(8,128)S(1)}, f32[]{:T(128)}) conditional(s32[]{:T(128)} %convert_element_type.22, (s32[]{:T(128)}, f32[1024,1024]{1,0:T(8,128)}, bf16[2048,1024]{1,0:T(8,128)(2,1)}) %tuple.41, (bf16[256,2048]{1,0:T(8,128)(2,1)}, bf16[2048,1024]{1,0:T(8,128)(2,1)}, f32[1024,1024]{1,0:T(8,128)}, bf16[256,2048]{1,0:T(8,128)(2,1)}) %tuple.42), branch_computations={%region_1.2_spmd, %region_2.4_spmd} | conditional | flops 5370281984 | bytes 67108968 | solution.py:433
  197.1 3.9 %fusion.16 = f32[256,1024]{1,0:T(8,128)S(1)} fusion(bf16[256,2048]{1,0:T(8,128)(2,1)} %get-tuple-element.22, bf16[2048,1024]{1,0:T(8,128)(2,1)} %get-tuple-element.23), kind=kOutput, calls=%fused_computation.40 | convolution fusion | flops 1073741824 | bytes 6291456 | tf_op jit(solution)/shard_map/cond/branch_1_fun/dot_general | solution.py:409
  201.1 1.3 fusion.18
  203.3 2.2 fusion.19
  205.5 2.2 fusion.17
  207.6 1.2 multiply_reduce_fusion
  210.1 5.9 %shard_map.49 = f32[8,128]{1,0:T(8,128)} custom-call(f32[8,128]{1,0:T(8,128)} %broadcast_in_dim.77.value_ref), custom_call_target="tpu_custom_call" | custom-call | tf_op jit(solution)/shard_map/pallas_call | solution.py:303
  217.9 1.5 multiply_bitcast_fusion
  (29 shorter events, 8.7 us)
Async XLA Ops:
  0.0 9.0 %collective-permute-start = (bf16[256,2048]{1,0:T(8,128)(2,1)}, bf16[256,2048]{1,0:T(8,128)(2,1)S(1)}, u32[]{:S(2)}, u32[]{:S(2)}) collective-permute-start(bf16[256,2048]{1,0:T(8,128)(2,1)} %bitcast.62), channel_id=1, source_target_pairs={{0,4},{4,0},{8,12},{12,8},{16,20},{20,16},{24,28},{28,24},{1,5},{5... | collective-permute-start | bytes 3145736 | tf_op jit(solution)/shard_map/ppermute | solution.py:14
  55.0 3.6 %copy-start.5 = (bf16[4,2,128,2048]{3,2,1,0:T(8,128)(2,1)S(1)}, bf16[4,2,128,2048]{3,2,1,0:T(8,128)(2,1)}, u32[]{:S(2)}) copy-start(bf16[4,2,128,2048]{3,2,1,0:T(8,128)(2,1)} %get-tuple-element.30) | copy-start | bytes 12582916
  58.7 2.2 copy-start.3
  60.0 2.7 %copy-start.2 = (f32[256,2048]{1,0:T(8,128)}, f32[256,2048]{1,0:T(8,128)S(1)}, u32[]{:S(2)}) copy-start(f32[256,2048]{1,0:T(8,128)S(1)} %convolution_select_fusion.1) | copy-start | bytes 6291460
  197.1 3.9 %copy-start.1 = (bf16[2048,1024]{1,0:T(8,128)(2,1)S(1)}, bf16[2048,1024]{1,0:T(8,128)(2,1)}, u32[]{:S(2)}) copy-start(bf16[2048,1024]{1,0:T(8,128)(2,1)} %get-tuple-element.23) | copy-start | bytes 12582916 | tf_op jit(solution)/shard_map/cond
  197.1 4.0 %copy-start.4 = (bf16[256,2048]{1,0:T(8,128)(2,1)S(1)}, bf16[256,2048]{1,0:T(8,128)(2,1)}, u32[]{:S(2)}) copy-start(bf16[256,2048]{1,0:T(8,128)(2,1)} %get-tuple-element.25) | copy-start | bytes 3145732 | tf_op jit(solution)/shard_map/cond
  201.1 2.2 copy-start

commit v3 on v2

--- a/solution.py
+++ b/solution.py
@@ -58,16 +58,32 @@
     return jnp.concatenate(rows, axis=0)
 
 
-def factor_kernel(gram_ref, out_ref, right_ref):
-    size = gram_ref.shape[0]
+def turned(x):
+    return x.astype(jnp.float32).T.astype(x.dtype)
+
+
+def factor_kernel(bounds_ref, rows_ref, out_ref, right_ref):
+    size = out_ref.shape[0]
     count = size // BLOCK
-
-    def copy(i, carry):
-        here = pl.ds(pl.multiple_of(i * BLOCK, BLOCK), BLOCK)
-        out_ref[here, :] = gram_ref[here, :]
-        return carry
-
-    lax.fori_loop(0, count, copy, 0)
+    wide = 2 * BLOCK
+    for i in range(size // wide):
+        left = turned(rows_ref[:, i * wide : (i + 1) * wide])
+        out_ref[i * wide : (i + 1) * wide, i * wide :] = jnp.dot(
+            left, rows_ref[:, i * wide :], preferred_element_type=jnp.float32
+        )
+    across = lax.broadcasted_iota(jnp.int32, (BLOCK, BLOCK), 1)
+    eye = lax.broadcasted_iota(jnp.int32, (BLOCK, BLOCK), 0) == across
+    kept = bounds_ref[1]
+    diagonal = jnp.zeros((BLOCK, BLOCK), jnp.float32)
+    for i in range(count):
+        here = slice(i * BLOCK, (i + 1) * BLOCK)
+        diagonal = diagonal + jnp.where(eye, out_ref[here, here], 0.0)
+    trace = jnp.sum(jnp.sum(diagonal, axis=0, keepdims=True), axis=1, keepdims=True)
+    ridge = ridge_ratio * trace / jnp.full((1, 1), kept, jnp.int32).astype(jnp.float32)
+    for i in range(count):
+        here = slice(i * BLOCK, (i + 1) * BLOCK)
+        added = jnp.where(across + i * BLOCK < kept, jnp.broadcast_to(ridge, eye.shape), 1.0)
+        out_ref[here, here] = out_ref[here, here] + jnp.where(eye, added, 0.0)
 
     def panel(k, carry):
         here = pl.ds(pl.multiple_of(k * BLOCK, BLOCK), BLOCK)
@@ -85,18 +101,27 @@
         right_ref[BLOCK : 2 * BLOCK, :] = low
         right_ref[2 * BLOCK : 3 * BLOCK, :] = high
 
-        def trailing(i, inner):
-            there = pl.ds(pl.multiple_of(i * BLOCK, BLOCK), BLOCK)
+        def trailing(first, height):
+            there = pl.ds(pl.multiple_of(first * BLOCK, BLOCK), height)
             left_high, left_low = halves(out_ref[here, there].T)
-            out_ref[there, here] = jnp.zeros((BLOCK, BLOCK), jnp.float32)
+            out_ref[there, here] = jnp.zeros((height, BLOCK), jnp.float32)
             out_ref[there, :] = out_ref[there, :] - jnp.dot(
                 jnp.concatenate([left_high, left_high, left_low], axis=1),
                 right_ref[...],
                 preferred_element_type=jnp.float32,
             )
+
+        odd = (count - 1 - k) % 2
+
+        @pl.when(odd == 1)
+        def _():
+            trailing(k + 1, BLOCK)
+
+        def pair(i, inner):
+            trailing(k + 1 + odd + 2 * i, wide)
             return inner
 
-        lax.fori_loop(k + 1, count, trailing, 0)
+        lax.fori_loop(0, (count - 1 - k) // 2, pair, 0)
         column = lax.broadcasted_iota(jnp.int32, (BLOCK, size), 1)
         out_ref[here, :] = jnp.where(column < (k + 1) * BLOCK, out_ref[here, :], 0.0)
         return carry
@@ -104,15 +129,89 @@
     lax.fori_loop(0, count, panel, 0)
 
 
-def factor_inverse(shifted):
-    size = shifted.shape[0]
+def factor_inverse(bounds, rows):
+    size = rows.shape[1]
     return pl.pallas_call(
         factor_kernel,
         out_shape=jax.ShapeDtypeStruct((size, size), jnp.float32),
-        in_specs=[pl.BlockSpec(memory_space=pltpu.VMEM)],
+        in_specs=[pl.BlockSpec(memory_space=pltpu.SMEM), pl.BlockSpec(memory_space=pltpu.VMEM)],
         out_specs=pl.BlockSpec(memory_space=pltpu.VMEM),
         scratch_shapes=[pltpu.VMEM((3 * BLOCK, size), jnp.bfloat16)],
-    )(shifted)
+    )(bounds, rows)
+
+
+CHUNK = 256
+
+
+def theta_kernel(gate_ref, bounds_ref, a_ref, b_ref, start_ref, theta_ref, own_ref, image_ref):
+    width = start_ref.shape[1]
+    height = a_ref.shape[0]
+    kept_right, kept_mid, first = bounds_ref[0], bounds_ref[1], bounds_ref[2]
+    lane = lax.broadcasted_iota(jnp.int32, (height, CHUNK), 1)
+
+    def mix(c, carry):
+        offset = c * CHUNK
+        inside = lane + offset < kept_right
+        mixed = []
+        for i in range(2):
+            for j in range(2):
+                columns = pl.ds(pl.multiple_of(j * width + offset, CHUNK), CHUNK)
+                product = jnp.dot(
+                    a_ref[:, i * width : (i + 1) * width],
+                    b_ref[:, columns],
+                    preferred_element_type=jnp.float32,
+                )
+                mixed.append(jnp.where(inside, product, 0.0))
+        for o in range(2):
+            for q in range(2):
+                row = 4 * (2 * o + q)
+                value = (
+                    gate_ref[row] * mixed[0]
+                    + gate_ref[row + 1] * mixed[1]
+                    + gate_ref[row + 2] * mixed[2]
+                    + gate_ref[row + 3] * mixed[3]
+                )
+                columns = pl.ds(pl.multiple_of(q * width + offset, CHUNK), CHUNK)
+                theta_ref[o, :, columns] = value.astype(jnp.bfloat16)
+        return carry
+
+    lax.fori_loop(0, width // CHUNK, mix, 0)
+
+    def image(c, carry):
+        columns = pl.ds(pl.multiple_of(c * CHUNK, CHUNK), CHUNK)
+        total = jnp.dot(
+            theta_ref[first, :, :width], start_ref[0, :, columns], preferred_element_type=jnp.float32
+        ) + jnp.dot(
+            theta_ref[first, :, width:], start_ref[1, :, columns], preferred_element_type=jnp.float32
+        )
+        image_ref[:, columns] = jnp.where(lane + c * CHUNK < kept_mid, total, 0.0).astype(jnp.bfloat16)
+        return carry
+
+    lax.fori_loop(0, width // CHUNK, image, 0)
+
+    def term(c, carry):
+        columns = pl.ds(pl.multiple_of(c * CHUNK, CHUNK), CHUNK)
+        own_ref[columns, :] = jnp.dot(
+            turned(theta_ref[first, :, columns]), image_ref[...], preferred_element_type=jnp.float32
+        ).astype(jnp.bfloat16)
+        return carry
+
+    lax.fori_loop(0, 2 * width // CHUNK, term, 0)
+
+
+def theta_terms(gate, bounds, a_used, b_full, starts):
+    height, wide = a_used.shape
+    width = starts.shape[2]
+    return pl.pallas_call(
+        theta_kernel,
+        out_shape=(
+            jax.ShapeDtypeStruct((2, height, wide), jnp.bfloat16),
+            jax.ShapeDtypeStruct((wide, width), jnp.bfloat16),
+        ),
+        in_specs=[pl.BlockSpec(memory_space=pltpu.SMEM)] * 2 + [pl.BlockSpec(memory_space=pltpu.VMEM)] * 3,
+        out_specs=(pl.BlockSpec(memory_space=pltpu.VMEM),) * 2,
+        scratch_shapes=[pltpu.VMEM((height, width), jnp.bfloat16)],
+    )(gate, bounds, a_used, b_full, starts)
 
 
 MESH = pl.DeviceIdType.MESH
@@ -329,7 +428,6 @@
     columns = jnp.arange(rank_width)
     row_global = bond_index * local_rows + jnp.arange(local_rows)
     mid_keep = columns < bond_mid
-    right_keep = columns < bond_right
     other_rows = partner(own_site, "chain", 0)
     a_rows = jnp.where(is_left, own_site, other_rows)
     b_rows = jnp.where(is_left, other_rows, own_site)
@@ -343,44 +441,10 @@
         starts = jnp.stack(
             [jnp.where(is_left, whole_start, other_start), jnp.where(is_left, other_start, whole_start)]
         )
-    start_zero, start_one = starts[0], starts[1]
     left_keep = (row_global < bond_left)[:, None] & jnp.tile(mid_keep, 2)[None, :]
     left_used = jnp.where(left_keep, a_rows, jnp.zeros((), jnp.bfloat16))
-    pair_keep = jnp.tile(right_keep, 2)[None, :]
-    mix_zero = jnp.where(
-        pair_keep,
-        jnp.dot(left_used[:, :rank_width], b_full, preferred_element_type=jnp.float32),
-        0.0,
-    )
-    mix_one = jnp.where(
-        pair_keep,
-        jnp.dot(left_used[:, rank_width:], b_full, preferred_element_type=jnp.float32),
-        0.0,
-    )
-    gate_matrix = gates[left_site].reshape(4, 4)
-
-    def theta_for(out_row):
-        gate_rows = lax.dynamic_slice_in_dim(gate_matrix, 2 * out_row, 2, 0)
-        pieces = []
-        for out_col in range(2):
-            coeffs = gate_rows[out_col]
-            pieces.append(
-                coeffs[0] * mix_zero[:, :rank_width]
-                + coeffs[1] * mix_zero[:, rank_width:]
-                + coeffs[2] * mix_one[:, :rank_width]
-                + coeffs[3] * mix_one[:, rank_width:]
-            )
-        return jnp.concatenate(pieces, axis=1).astype(jnp.bfloat16)
-
-    theta_rows = theta_for(jnp.where(is_left, 0, 1))
-    theta_second = theta_for(1)
-    image_full = jnp.dot(
-        theta_rows[:, :rank_width], start_zero, preferred_element_type=jnp.float32
-    ) + jnp.dot(theta_rows[:, rank_width:], start_one, preferred_element_type=jnp.float32)
-    image_rows = jnp.where(mid_keep[None, :], image_full, 0.0).astype(jnp.bfloat16)
-    own = lax.dot_general(
-        theta_rows, image_rows, (((0,), (0,)), ((), ())), preferred_element_type=jnp.float32
-    ).astype(jnp.bfloat16)
+    bounds = jnp.stack([bond_right, bond_mid, jnp.where(is_left, 0, 1)]).astype(jnp.int32)
+    thetas, own = theta_terms(gates[left_site], bounds, left_used, b_full, starts)
     if square:
         projected_all = reduce_pair(own)
     else:
@@ -395,28 +459,20 @@
         projected_all = jnp.concatenate(
             [jnp.where(is_left, own_half, other_half), jnp.where(is_left, other_half, own_half)], axis=0
         )
-    gram = lax.dot_general(
-        projected_all, projected_all, (((0,), (0,)), ((), ())), preferred_element_type=jnp.float32
-    )
-    eye = jnp.arange(rank_width)[:, None] == jnp.arange(rank_width)[None, :]
-    trace_sum = jnp.sum(jnp.where(eye, gram, 0.0))
-    added = jnp.where(mid_keep, ridge_ratio * trace_sum / bond_mid.astype(jnp.float32), 1.0)
-    inverse = factor_inverse(gram + jnp.where(eye, added[None, :], 0.0))
+    inverse = factor_inverse(bounds, projected_all)
 
     def left_rows():
-        pieces = []
-        for theta in (theta_rows, theta_second):
-            reduced = jnp.dot(theta, projected_all, preferred_element_type=jnp.float32)
-            pieces.append(
-                lax.dot_general(
-                    reduced,
-                    inverse,
-                    (((1,), (1,)), ((), ())),
-                    precision=lax.Precision.HIGH,
-                    preferred_element_type=jnp.float32,
-                )
-            )
-        joined = jnp.concatenate(pieces, axis=1)
+        reduced = jnp.dot(
+            thetas.reshape(2 * local_rows, -1), projected_all, preferred_element_type=jnp.float32
+        )
+        upper = lax.dot_general(
+            reduced,
+            inverse,
+            (((1,), (1,)), ((), ())),
+            precision=lax.Precision.HIGH,
+            preferred_element_type=jnp.float32,
+        )
+        joined = jnp.concatenate([upper[:local_rows], upper[local_rows:]], axis=1)
         return joined, jnp.sum(joined * joined)
 
     def right_rows():

time: 220 us -> 186 us (0.85)
  matrix products: 32.3 us -> 9.01 us
  other arithmetic: 27.1 us -> 9.2 us
  Pallas kernels: 145 us -> 160 us
  local copies, waits for them, and re-layouts: 10.3 us -> 3.89 us
    dot_general x7 -> x1, matrix products: 28 us -> 5.29 us  [left_rows(): jnp.dot(thetas.reshape(2 * local_rows, -1), projected_all, preferred_elem...]
    pallas_call x0 -> x1, Pallas kernels: none -> 14.7 us  [theta_terms(): pl.pallas_call(theta_kernel, out_shape=(jax.ShapeDtypeStruct((2, height,...]
    slice x1 -> x0, other arithmetic: 5.38 us -> none  [local(): theta_rows[:, rank_width:]]
    another operation x1, other arithmetic: 7.14 us -> 1.93 us  [local(): jnp.stack([bond_right, bond_mid, jnp.where(is_left, 0, 1)])]
    add x1 -> x0, other arithmetic: 5.01 us -> none  [local(): inverse = factor_inverse(gram + jnp.where(eye, added[None, :], 0.0))]
    slice x3 -> x1, local copies, waits for them, and re-layouts: 3.17 us -> 0.14 us  [left_rows(): joined = jnp.concatenate([upper[:local_rows], upper[local_rows:]], axis=1)]
where the time goes in v3:
time: 186 us
  Pallas kernels  160 us (86%)
  other arithmetic  9.2 us (5%)
  matrix products  9.01 us (5%)
  local copies, waits for them, and re-layouts  3.89 us (2%)
  between operations  2.7 us (1%)
    pallas_call x1, Pallas kernels, factor_inverse(): pl.pallas_call(factor_kernel, out_shape=jax.ShapeDtypeStruct((size, size)...  50.2 us
    pallas_call x1, Pallas kernels, reduce_pair(): pl.pallas_call(reduce_kernel, out_shape=jax.ShapeDtypeStruct((2, n, rows,...  46.1 us
    pallas_call x1, Pallas kernels, gather_pair(): pl.pallas_call(gather_kernel, out_shape=(jax.ShapeDtypeStruct((n, 2, rows...  43.1 us
    pallas_call x1, Pallas kernels, theta_terms(): pl.pallas_call(theta_kernel, out_shape=(jax.ShapeDtypeStruct((2, height,...  14.7 us
    pallas_call x1, Pallas kernels, total_of(): pl.pallas_call(total_kernel, out_shape=jax.ShapeDtypeStruct(shape, jnp.fl...  5.93 us
    dot_general x1, matrix products, left_rows(): jnp.dot(thetas.reshape(2 * local_rows, -1), projected_all, preferred_elem...  5.29 us
  transfers between devices with their start and end apart: 1, of which 0 were waited for; matrix products, arithmetic and copies ran while one was open for 3% of the time, Pallas kernels for 0%

profile of v3, /device:TPU:0, one launch (start us, length us, event | category | flops | bytes accessed | tf_op | source)
XLA Modules:
  0.0 186.0 jit_solution(2914058124731939942)
XLA Ops:
  0.0 0.0 copy-start
  0.0 0.5 collective-permute-start
  0.5 1.4 fusion.4
  3.8 0.6 iota_compare_fusion
  4.5 0.6 add_compare_fusion
  5.2 1.9 %pad_add_fusion.bounds_ref = s32[3]{0:T(128)} fusion(s32[1]{0:T(128)} %bitcast.1, s32[1]{0:T(128)} %get-tuple-element.43, s32[1]{0:T(128)} %get-tuple-element.42), kind=kLoop, calls=%fused_computation.10 | loop fusion | flops 6 | bytes 24 | tf_op jit(solution)/shard_map/stack | solution.py:446
  7.1 0.0 copy-done
  7.1 0.5 dynamic-slice_bitcast_fusion.gate_ref
  7.6 0.0 collective-permute-done
  7.6 3.3 %broadcast_select_fusion = (bf16[256,2048]{1,0:T(8,128)(2,1)}, bf16[256,2048]{1,0:T(8,128)(2,1)}) fusion(bf16[256,2048]{1,0:T(8,128)(2,1)S(1)} %collective-permute-done, pred[]{:T(512)S(6)} %eq.5, bf16[1,256,2048]{2,1,0:T(8,128)(2,1)} %param.6, pred[2048]{0:T(1024)(128)(4,1)S(1)} %and.24, pred[256]{0:T(512)(128)(4,1)S(1)} %add_compare_fusion), kind=kLoop, calls=%fused_computation.7 | loop fusion | flops 2097152 | bytes 4196609 | tf_op jit(solution)/shard_map/jit(_where)/select_n | solution.py:433
  11.0 43.1 %shard_map.46 = (bf16[4,2,128,2048]{3,2,1,0:T(8,128)(2,1)}, bf16[2,4,256,1024]{3,2,1,0:T(8,128)(2,1)}) custom-call(bf16[2,128,2048]{2,1,0:T(8,128)(2,1)} %bitcast.30, bf16[256,1024]{1,0:T(8,128)(2,1)} %bitcast.32), custom_call_target="tpu_custom_call" | custom-call | tf_op jit(solution)/shard_map/pallas_call | solution.py:300
  54.1 14.7 %shard_map.47 = (bf16[2,256,2048]{2,1,0:T(8,128)(2,1)}, bf16[2048,1024]{1,0:T(8,128)(2,1)}) custom-call(f32[16]{0:T(128)} %dynamic-slice_bitcast_fusion.gate_ref, s32[3]{0:T(128)} %pad_add_fusion.bounds_ref, bf16[256,2048]{1,0:T(8,128)(2,1)} %get-tuple-element.40.a_ref, bf16[1024,2048]{1,0:T(8,128)(2,1)} %bitcast.27, bf16[2,1024,1024]{2,1,0:T(8,128)(2,1)} %bitcast.28), custom_call_target="tpu_custom_call" | custom-call | tf_op jit(solution)/shard_map/pallas_call | solution.py:205
  68.8 46.1 %shard_map.48 = bf16[2,4,256,1024]{3,2,1,0:T(8,128)(2,1)} custom-call(bf16[2,4,256,1024]{3,2,1,0:T(8,128)(2,1)} %bitcast.29), custom_call_target="tpu_custom_call" | custom-call | tf_op jit(solution)/shard_map/pallas_call | solution.py:371
  114.9 50.2 %shard_map.49 = f32[1024,1024]{1,0:T(8,128)} custom-call(s32[3]{0:T(128)} %pad_add_fusion.bounds_ref, bf16[2048,1024]{1,0:T(8,128)(2,1)} %bitcast.24), custom_call_target="tpu_custom_call" | custom-call | tf_op jit(solution)/shard_map/pallas_call | solution.py:134
  165.0 11.1 %conditional.1 = (f32[256,2048]{1,0:T(8,128)S(1)}, f32[]{:T(128)}) conditional(s32[]{:T(128)} %convert_element_type.14, (s32[]{:T(128)}, f32[1024,1024]{1,0:T(8,128)}, bf16[2048,1024]{1,0:T(8,128)(2,1)}) %tuple.22, (bf16[2,256,2048]{2,1,0:T(8,128)(2,1)}, bf16[2048,1024]{1,0:T(8,128)(2,1)}, f32[1024,1024]{1,0:T(8,128)}) %tuple.23), branch_computations={%region_0.1_spmd, %region_1.3_spmd} | conditional | flops 5370281984 | bytes 41943088 | solution.py:489
  165.0 5.3 %fusion.5 = f32[512,1024]{1,0:T(8,128)S(1)} fusion(bf16[512,2048]{1,0:T(8,128)(2,1)} %bitcast.33, bf16[2048,1024]{1,0:T(8,128)(2,1)} %get-tuple-element.21), kind=kOutput, calls=%fused_computation.14 | convolution fusion | flops 2147483648 | bytes 8388608 | tf_op jit(solution)/shard_map/cond/branch_1_fun/dot_general | solution.py:465
  170.3 0.0 copy-done.1
  170.4 3.7 %fusion.6 = f32[512,1024]{1,0:T(8,128)S(1)} fusion(f32[512,1024]{1,0:T(8,128)S(1)} %fusion.5, f32[1024,1024]{1,0:T(8,128)S(1)} %copy-done.1), kind=kOutput, calls=%fused_computation.15 | convolution fusion | flops 3221225472 | bytes 8388608 | tf_op jit(solution)/shard_map/cond/branch_1_fun/dot_general | solution.py:468
  174.1 0.1 fusion.3
  174.2 1.2 multiply_reduce_fusion
  176.1 0.6 broadcast_in_dim.12.value_ref
  176.7 5.9 %shard_map.50 = f32[8,128]{1,0:T(8,128)} custom-call(f32[8,128]{1,0:T(8,128)} %broadcast_in_dim.12.value_ref), custom_call_target="tpu_custom_call" | custom-call | tf_op jit(solution)/shard_map/pallas_call | solution.py:402
  182.6 1.2 slice.9
  184.5 1.5 multiply_bitcast_fusion
  (3 shorter events, 0.0 us)
Async XLA Ops:
  0.0 7.1 %copy-start = (f32[8,16]{1,0:T(8,128)S(1)}, f32[8,16]{1,0:T(8,128)}, u32[]{:S(2)}) copy-start(f32[8,16]{1,0:T(8,128)} %param.8) | copy-start | bytes 1540
  0.0 7.6 %collective-permute-start = (bf16[256,2048]{1,0:T(8,128)(2,1)}, bf16[256,2048]{1,0:T(8,128)(2,1)S(1)}, u32[]{:S(2)}, u32[]{:S(2)}) collective-permute-start(bf16[256,2048]{1,0:T(8,128)(2,1)} %bitcast.31), channel_id=1, source_target_pairs={{0,4},{4,0},{8,12},{12,8},{16,20},{20,16},{24,28},{28,24},{1,5},{5... | collective-permute-start | bytes 3145736 | tf_op jit(solution)/shard_map/ppermute | solution.py:14
  165.0 5.3 %copy-start.1 = (f32[1024,1024]{1,0:T(8,128)S(1)}, f32[1024,1024]{1,0:T(8,128)}, u32[]{:S(2)}) copy-start(f32[1024,1024]{1,0:T(8,128)} %get-tuple-element.22) | copy-start | bytes 12582916 | tf_op jit(solution)/shard_map/cond

commit v4 on v3

--- a/solution.py
+++ b/solution.py
@@ -410,7 +410,7 @@
             pltpu.SemaphoreType.DMA((3,)),
         ],
         compiler_params=pltpu.CompilerParams(collective_id=2, has_side_effects=True),
-    )(jnp.full(shape, value, jnp.float32))[0, 0]
+    )(jnp.full(shape, value, jnp.float32))[:1, :1]
 
 
 def local(sites, start, gates, bonds):
@@ -492,7 +492,7 @@
         sum_squares / (2.0 * bond_left.astype(jnp.float32) * bond_mid.astype(jnp.float32)) + 1e-06
     )
     factor = jnp.where(
-        is_left, lax.rsqrt(mean_square), jnp.sqrt(2.0 * bond_right.astype(jnp.float32))
+        jnp.full(jnp.shape(mean_square), is_left), lax.rsqrt(mean_square), jnp.sqrt(2.0 * bond_right.astype(jnp.float32))
     )
     return (rows * factor)[None]
 

time: 186 us -> 186 us (level)
  no operation moved by 1% of the time
where the time goes in v4:
time: 186 us
  Pallas kernels  160 us (86%)
  other arithmetic  9.2 us (5%)
  matrix products  9.01 us (5%)
  local copies, waits for them, and re-layouts  3.9 us (2%)
  between operations  2.7 us (1%)
    pallas_call x1, Pallas kernels, factor_inverse(): pl.pallas_call(factor_kernel, out_shape=jax.ShapeDtypeStruct((size, size)...  50.2 us
    pallas_call x1, Pallas kernels, reduce_pair(): pl.pallas_call(reduce_kernel, out_shape=jax.ShapeDtypeStruct((2, n, rows,...  46.1 us
    pallas_call x1, Pallas kernels, gather_pair(): pl.pallas_call(gather_kernel, out_shape=(jax.ShapeDtypeStruct((n, 2, rows...  43.1 us
    pallas_call x1, Pallas kernels, theta_terms(): pl.pallas_call(theta_kernel, out_shape=(jax.ShapeDtypeStruct((2, height,...  14.7 us
    pallas_call x1, Pallas kernels, total_of(): pl.pallas_call(total_kernel, out_shape=jax.ShapeDtypeStruct(shape, jnp.fl...  5.93 us
    dot_general x1, matrix products, left_rows(): jnp.dot(thetas.reshape(2 * local_rows, -1), projected_all, preferred_elem...  5.29 us
  transfers between devices with their start and end apart: 1, of which 0 were waited for; matrix products, arithmetic and copies ran while one was open for 3% of the time, Pallas kernels for 0%

profile of v4, /device:TPU:0, one launch (start us, length us, event | category | flops | bytes accessed | tf_op | source)
XLA Modules:
  0.0 186.0 jit_solution(8413071033080568387)
XLA Ops:
  0.0 0.0 copy-start
  0.0 0.5 collective-permute-start
  0.5 1.4 fusion.4
  3.8 0.6 iota_compare_fusion
  4.5 0.6 add_compare_fusion
  5.2 1.9 %pad_add_fusion.bounds_ref = s32[3]{0:T(128)} fusion(s32[1]{0:T(128)} %bitcast.1, s32[1]{0:T(128)} %get-tuple-element.43, s32[1]{0:T(128)} %get-tuple-element.42), kind=kLoop, calls=%fused_computation.10 | loop fusion | flops 6 | bytes 24 | tf_op jit(solution)/shard_map/stack | solution.py:446
  7.1 0.0 copy-done
  7.1 0.5 dynamic-slice_bitcast_fusion.gate_ref
  7.6 0.0 collective-permute-done
  7.6 3.3 %broadcast_select_fusion = (bf16[256,2048]{1,0:T(8,128)(2,1)}, bf16[256,2048]{1,0:T(8,128)(2,1)}) fusion(bf16[256,2048]{1,0:T(8,128)(2,1)S(1)} %collective-permute-done, pred[]{:T(512)} %eq.5, bf16[1,256,2048]{2,1,0:T(8,128)(2,1)} %param.6, pred[2048]{0:T(1024)(128)(4,1)S(1)} %and.24, pred[256]{0:T(512)(128)(4,1)S(1)} %add_compare_fusion), kind=kLoop, calls=%fused_computation.7 | loop fusion | flops 2097152 | bytes 4196609 | tf_op jit(solution)/shard_map/jit(_where)/select_n | solution.py:433
  11.0 43.1 %shard_map.46 = (bf16[4,2,128,2048]{3,2,1,0:T(8,128)(2,1)}, bf16[2,4,256,1024]{3,2,1,0:T(8,128)(2,1)}) custom-call(bf16[2,128,2048]{2,1,0:T(8,128)(2,1)} %bitcast.32, bf16[256,1024]{1,0:T(8,128)(2,1)} %bitcast.34), custom_call_target="tpu_custom_call" | custom-call | tf_op jit(solution)/shard_map/pallas_call | solution.py:300
  54.1 14.7 %shard_map.47 = (bf16[2,256,2048]{2,1,0:T(8,128)(2,1)}, bf16[2048,1024]{1,0:T(8,128)(2,1)}) custom-call(f32[16]{0:T(128)} %dynamic-slice_bitcast_fusion.gate_ref, s32[3]{0:T(128)} %pad_add_fusion.bounds_ref, bf16[256,2048]{1,0:T(8,128)(2,1)} %get-tuple-element.40.a_ref, bf16[1024,2048]{1,0:T(8,128)(2,1)} %bitcast.29, bf16[2,1024,1024]{2,1,0:T(8,128)(2,1)} %bitcast.30), custom_call_target="tpu_custom_call" | custom-call | tf_op jit(solution)/shard_map/pallas_call | solution.py:205
  68.8 46.1 %shard_map.48 = bf16[2,4,256,1024]{3,2,1,0:T(8,128)(2,1)} custom-call(bf16[2,4,256,1024]{3,2,1,0:T(8,128)(2,1)} %bitcast.31), custom_call_target="tpu_custom_call" | custom-call | tf_op jit(solution)/shard_map/pallas_call | solution.py:371
  114.9 50.2 %shard_map.49 = f32[1024,1024]{1,0:T(8,128)} custom-call(s32[3]{0:T(128)} %pad_add_fusion.bounds_ref, bf16[2048,1024]{1,0:T(8,128)(2,1)} %bitcast.26), custom_call_target="tpu_custom_call" | custom-call | tf_op jit(solution)/shard_map/pallas_call | solution.py:134
  165.0 11.1 %conditional.1 = (f32[256,2048]{1,0:T(8,128)S(1)}, f32[]{:T(128)}) conditional(s32[]{:T(128)} %convert_element_type.14, (s32[]{:T(128)}, f32[1024,1024]{1,0:T(8,128)}, bf16[2048,1024]{1,0:T(8,128)(2,1)}) %tuple.22, (bf16[2,256,2048]{2,1,0:T(8,128)(2,1)}, bf16[2048,1024]{1,0:T(8,128)(2,1)}, f32[1024,1024]{1,0:T(8,128)}) %tuple.23), branch_computations={%region_0.1_spmd, %region_1.3_spmd} | conditional | flops 5370281984 | bytes 41943088 | solution.py:489
  165.0 5.3 %fusion.5 = f32[512,1024]{1,0:T(8,128)S(1)} fusion(bf16[512,2048]{1,0:T(8,128)(2,1)} %bitcast.35, bf16[2048,1024]{1,0:T(8,128)(2,1)} %get-tuple-element.21), kind=kOutput, calls=%fused_computation.14 | convolution fusion | flops 2147483648 | bytes 8388608 | tf_op jit(solution)/shard_map/cond/branch_1_fun/dot_general | solution.py:465
  170.3 0.0 copy-done.1
  170.4 3.7 %fusion.6 = f32[512,1024]{1,0:T(8,128)S(1)} fusion(f32[512,1024]{1,0:T(8,128)S(1)} %fusion.5, f32[1024,1024]{1,0:T(8,128)S(1)} %copy-done.1), kind=kOutput, calls=%fused_computation.15 | convolution fusion | flops 3221225472 | bytes 8388608 | tf_op jit(solution)/shard_map/cond/branch_1_fun/dot_general | solution.py:468
  174.1 0.1 fusion.3
  174.2 1.2 multiply_reduce_fusion
  176.1 0.6 broadcast_in_dim.20.value_ref
  176.7 5.9 %shard_map.50 = f32[8,128]{1,0:T(8,128)} custom-call(f32[8,128]{1,0:T(8,128)} %broadcast_in_dim.20.value_ref), custom_call_target="tpu_custom_call" | custom-call | tf_op jit(solution)/shard_map/pallas_call | solution.py:402
  182.6 1.2 slice.9
  184.5 1.5 multiply_bitcast_fusion
  (3 shorter events, 0.0 us)
Async XLA Ops:
  0.0 7.1 %copy-start = (f32[8,16]{1,0:T(8,128)S(1)}, f32[8,16]{1,0:T(8,128)}, u32[]{:S(2)}) copy-start(f32[8,16]{1,0:T(8,128)} %param.8) | copy-start | bytes 1540
  0.0 7.6 %collective-permute-start = (bf16[256,2048]{1,0:T(8,128)(2,1)}, bf16[256,2048]{1,0:T(8,128)(2,1)S(1)}, u32[]{:S(2)}, u32[]{:S(2)}) collective-permute-start(bf16[256,2048]{1,0:T(8,128)(2,1)} %bitcast.33), channel_id=1, source_target_pairs={{0,4},{4,0},{8,12},{12,8},{16,20},{20,16},{24,28},{28,24},{1,5},{5... | collective-permute-start | bytes 3145736 | tf_op jit(solution)/shard_map/ppermute | solution.py:14
  165.0 5.3 %copy-start.1 = (f32[1024,1024]{1,0:T(8,128)S(1)}, f32[1024,1024]{1,0:T(8,128)}, u32[]{:S(2)}) copy-start(f32[1024,1024]{1,0:T(8,128)} %get-tuple-element.22) | copy-start | bytes 12582916 | tf_op jit(solution)/shard_map/cond
